TPU v7x, 128 devices: a whole 4x4x4 slice. The times are simulated.
128 devices in a mesh: grp: 4 (over x_lo, core), seq: 32 (over x_hi, z, y).
Axes of the slice: x: 4 (x_hi: 2, x_lo: 2; x = x_hi * 2 + x_lo), y: 4, z: 4, core: 2. Of those that a mesh axis runs over, the one named last changes fastest.
Arguments:
- patches: bfloat16 [8192, 1280], P(('grp', 'seq')), may hold values from -60 to 60
- piece_ids: int32 [128, 64], P(('grp', 'seq')), may hold values from 0 to 2, never falling along the last dimension, each value on 1 to 48 neighbouring positions
- vit_gain: float32 [1280], replicated, may hold values from 0.25 to 1.75
- vit_qkv: bfloat16 [1280, 3840], replicated
- vit_out: bfloat16 [1280, 1280], replicated, may hold values from -0.15625 to 0.15625
- merge_gain: float32 [1280], replicated, may hold values from 0.25 to 1.75
- merge_up: bfloat16 [5120, 5120], P(None, 'seq'), may hold values from -0.078125 to 0.078125
- merge_down: bfloat16 [5120, 8192], P(None, 'seq'), may hold values from -0.078125 to 0.078125
- dest: int32 [2048], P(('grp', 'seq')), may hold values from 0 to 31, as said below
- tokens: bfloat16 [32768, 8192], P(('grp', 'seq')), may hold values from -60 to 60
- image_index: int32 [32768], P(('grp', 'seq')), may hold values from 0 to 32, as said below
- doc_lengths: int32 [4, 4], P('grp'), may hold values from 1 to 4096, 8192 in all within a row
- attn_gain: float32 [8192], replicated, may hold values from 0.25 to 1.75
- attn_qkv: bfloat16 [8192, 768], P(('grp', 'seq'))
- attn_out: bfloat16 [512, 8192], P(None, ('grp', 'seq')), may hold values from -0.25 to 0.25
Outputs:
- layer_out: bfloat16 [32768, 8192], P(('grp', 'seq'))
Inputs may be any that keep to these rules, and one draw needn't show every extreme that they name: `dest`: within each aligned block of 16 rows (one device's merged rows), exactly 16 distinct values occur, each exactly 1 times, and in every group one device is named by every device of the group. `image_index`: 32 marks a text token. A value k < 32 on a device names the merged row that the device of seq index k // 1 in its group sends to it as its (k % 1)-th row in row order; each such row is named by exactly one token of the receiving device, and no other values occur. `piece_ids`: piece numbers never fall within a window. `doc_lengths`: each group's documents fill its 8192 positions.
All inputs are finite; a program needn't handle non-finite values.
Results may differ from a plain program's by a relative error of at most 0.0093.
The roundings to bfloat16 on the way count: a program that leaves them out, or rounds other values in their place, can miss the bound.
Values may be sent and summed in bfloat16 or wider, within the bound.
No kernel may reach another device: no remote copies, remote signals or barrier semaphores. Data moves between devices by JAX's collectives and lax.ppermute only.
A program may use at most 192 MiB of HBM per device.

v0:
```python
import jax
import jax.numpy as jnp
from jax import lax
from jax.sharding import Mesh
from jax.sharding import PartitionSpec as P

VHEADS = 16
WIN = 64
SEQ = ("seq_0", "seq_1", "seq_2")
GRP_SEQ = ("grp_0", "grp_1", "seq_0", "seq_1", "seq_2")
GRP = ("grp_0", "grp_1")


EPSILON = 1e-06


def cut_rows(length, count):
    lap = length // count
    if lap >= 8:
        lap -= lap % 8
    return [lap * k for k in range(1, count)]


def all_blocks(x, axes, turns):
    parts = x[None]
    for k in turns:
        parts = lax.all_gather(parts, axes[k], axis=0, tiled=True)
    current = [lax.axis_size(axes[k]) for k in reversed(turns)]
    parts = parts.reshape(*current, *x.shape)
    turned = sorted(range(len(turns)), key=lambda place: turns[len(turns) - 1 - place])
    return parts.transpose(*turned, *range(len(turns), parts.ndim)).reshape(-1, *x.shape)


def joined_along(parts, dim):
    parts = jnp.moveaxis(parts, 0, dim)
    shape = parts.shape
    return parts.reshape(*shape[:dim], shape[dim] * shape[dim + 1], *shape[dim + 2 :])


def gather_all_axes(x, axes, dim):
    widest = max(range(max(1, x.ndim - 1)), key=lambda d: x.shape[d])
    count, outs = (len(axes), [])
    for first, slab in enumerate(jnp.split(x, cut_rows(x.shape[widest], count), axis=widest)):
        if slab.size:
            turns = [(first - k) % count for k in range(count)]
            outs.append(all_blocks(slab, axes, turns))
    return joined_along(jnp.concatenate(outs, axis=widest + 1), dim)


def from_behind(value, axis, steps):
    count = lax.axis_size(axis)
    first, last = (max(0, -steps), min(count, count - steps))
    return lax.ppermute(value, axis, [(source, source + steps) for source in range(first, last)])


def rms_scale(inputs, gain):
    mean_square = jnp.mean(inputs * inputs, axis=-1, keepdims=True)
    return inputs * lax.rsqrt(mean_square + EPSILON) * gain


def softmax_mix(scores, allowed, value_collection, spec):
    scores = jnp.where(allowed[None], scores, -1e30)
    highest = jnp.max(scores, axis=-1, keepdims=True)
    weights = jnp.exp(scores - highest)
    totals = jnp.sum(weights, axis=-1)
    mixture = jnp.einsum(
        spec, weights.astype(jnp.bfloat16), value_collection, preferred_element_type=jnp.float32
    )
    return mixture / jnp.transpose(totals)[:, :, None]


def window_layer(patch_rows, piece_rows, vit_gain, vit_qkv, vit_out, merge_gain):
    row_count, features = patch_rows.shape
    head_dim = features // VHEADS
    residual = patch_rows.astype(jnp.float32)
    normed = rms_scale(residual, vit_gain).astype(jnp.bfloat16)
    projected = jnp.dot(normed, vit_qkv, preferred_element_type=jnp.float32).astype(jnp.bfloat16)
    queries = projected[:, :features].reshape(row_count, VHEADS, head_dim)
    key_set = projected[:, features : 2 * features].reshape(row_count, VHEADS, head_dim)
    value_collection = projected[:, 2 * features :].reshape(row_count, VHEADS, head_dim)
    scores = jnp.einsum(
        "qhd,khd->hqk", queries, key_set, preferred_element_type=jnp.float32
    ) * head_dim ** (-0.5)
    frames = jnp.arange(row_count, dtype=jnp.int32) // WIN
    allowed = (frames[:, None] == frames[None, :]) & (piece_rows[:, None] == piece_rows[None, :])
    mixture = softmax_mix(scores, allowed, value_collection, "hqk,khd->qhd")
    mixture = mixture.reshape(row_count, features).astype(jnp.bfloat16)
    residual = residual + jnp.dot(mixture, vit_out, preferred_element_type=jnp.float32)
    merge_input = rms_scale(residual, merge_gain).astype(jnp.bfloat16)
    return merge_input.reshape(row_count // 4, 4 * features)


def attend(query_rows, query_pos, query_start, key_value, key_pos):
    row_count = query_rows.shape[0]
    head_dim = key_value.shape[1] // 2
    heads = query_rows.shape[1] // head_dim
    queries = query_rows.reshape(row_count, heads, head_dim)
    scores = jnp.einsum(
        "qhd,kd->hqk", queries, key_value[:, :head_dim], preferred_element_type=jnp.float32
    ) * head_dim ** (-0.5)
    allowed = (key_pos[None, :] >= query_start[:, None]) & (key_pos[None, :] <= query_pos[:, None])
    mixture = softmax_mix(scores, allowed, key_value[:, head_dim:], "hqk,kd->qhd")
    return mixture.reshape(row_count, heads * head_dim).astype(jnp.bfloat16)


def slot_numbers(targets):
    row_count = targets.shape[-1]
    order = jnp.arange(row_count, dtype=jnp.int32)
    same = targets[..., :, None] == targets[..., None, :]
    earlier = order[None, :] < order[:, None]
    return jnp.sum(same & earlier, axis=-1)


def on_device(
    patches,
    piece_ids,
    vit_gain,
    vit_qkv,
    vit_out,
    merge_gain,
    merge_up,
    merge_down,
    dest,
    tokens,
    image_index,
    doc_lengths,
    attn_gain,
    attn_qkv,
    attn_out,
):
    features = patches.shape[1]
    block_len = WIN
    patch_blocks = patches.reshape(-1, block_len, features)
    merge_input = lax.map(
        lambda parts: window_layer(parts[0], parts[1], vit_gain, vit_qkv, vit_out, merge_gain),
        (patch_blocks, piece_ids),
    ).reshape(-1, 4 * features)
    own_rows = merge_input.shape[0]
    seq_count = lax.axis_size(SEQ)
    seq_index = lax.axis_index(SEQ)
    hidden_part = jax.nn.gelu(
        jnp.dot(
            lax.all_gather(merge_input, SEQ, axis=0, tiled=True),
            merge_up,
            preferred_element_type=jnp.float32,
        ),
        approximate=False,
    ).astype(jnp.bfloat16)
    column_part = jnp.dot(
        lax.all_gather(hidden_part, SEQ, axis=1, tiled=True),
        merge_down,
        preferred_element_type=jnp.float32,
    ).astype(jnp.bfloat16)
    capacity = own_rows // (seq_count // 2)
    slots = seq_count * capacity
    receivers = jnp.arange(seq_count, dtype=jnp.int32)
    slot_ids = jnp.arange(capacity, dtype=jnp.int32)
    home_rows = lax.all_to_all(column_part, SEQ, split_axis=0, concat_axis=1, tiled=True)
    order = slot_numbers(dest)
    select = (dest[None, None, :] == receivers[:, None, None]) & (
        order[None, None, :] == slot_ids[None, :, None]
    )
    outgoing = jnp.einsum(
        "dcj,jf->dcf", select.astype(jnp.bfloat16), home_rows, preferred_element_type=jnp.float32
    ).astype(jnp.bfloat16)
    arrived = lax.all_to_all(outgoing, SEQ, split_axis=0, concat_axis=0, tiled=True).reshape(
        slots, -1
    )
    slot_all = jnp.arange(slots, dtype=jnp.int32)
    picker = (image_index[:, None] == slot_all[None, :]).astype(jnp.bfloat16)
    pictured = jnp.dot(picker, arrived, preferred_element_type=jnp.float32).astype(jnp.bfloat16)
    layer_in = jnp.where((image_index < slots)[:, None], pictured, tokens)
    tok_rows = tokens.shape[0]
    normed = rms_scale(layer_in.astype(jnp.float32), attn_gain).astype(jnp.bfloat16)
    projected = jnp.dot(
        normed, gather_all_axes(attn_qkv, GRP_SEQ, 0), preferred_element_type=jnp.float32
    ).astype(jnp.bfloat16)
    query_width = attn_out.shape[0]
    queries = projected[:, :query_width]
    key_value = projected[:, query_width:]
    head_dim = key_value.shape[1] // 2
    head_count = query_width // head_dim
    positions = seq_index * tok_rows + jnp.arange(tok_rows, dtype=jnp.int32)
    lengths = doc_lengths[0]
    order_of = jnp.arange(lengths.shape[0], dtype=jnp.int32)
    starts = jnp.sum(jnp.where(order_of[None, :] < order_of[:, None], lengths[None, :], 0), axis=1)
    doc_start = jnp.max(
        jnp.where(starts[None, :] <= positions[:, None], starts[None, :], 0), axis=1
    )
    reach = seq_count // 2
    buffer = jnp.zeros(((reach + 1) * tok_rows, key_value.shape[1]), key_value.dtype)
    buffer = lax.dynamic_update_slice_in_dim(buffer, key_value, reach * tok_rows, 0)

    def step_back(turn, state):
        current, filled = state
        current = from_behind(current, SEQ, 1)
        filled = lax.dynamic_update_slice_in_dim(filled, current, (reach - turn) * tok_rows, 0)
        return (current, filled)

    key_rows = lax.fori_loop(1, reach + 1, step_back, (key_value, buffer))[1]
    key_pos = (seq_index - reach) * tok_rows + jnp.arange(key_rows.shape[0], dtype=jnp.int32)
    block_rows = min(tok_rows, 512)
    head_queries = queries.reshape(tok_rows, head_count, head_dim).transpose(1, 0, 2)

    def one_head(head_rows):
        return lax.map(
            lambda parts: attend(parts[0], parts[1], parts[2], key_rows, key_pos),
            (
                head_rows.reshape(-1, block_rows, head_dim),
                positions.reshape(-1, block_rows),
                doc_start.reshape(-1, block_rows),
            ),
        ).reshape(tok_rows, head_dim)

    attended = lax.map(one_head, head_queries).transpose(1, 0, 2).reshape(tok_rows, query_width)
    update = jnp.dot(
        attended,
        lax.all_gather(attn_out, GRP_SEQ, axis=1, tiled=True),
        preferred_element_type=jnp.float32,
    )
    return (layer_in.astype(jnp.float32) + update).astype(jnp.bfloat16)


def solution(mesh):
    torus = Mesh(mesh.devices.reshape(2, 2, 2, 4, 4), ("grp_0", "grp_1", "seq_0", "seq_1", "seq_2"))
    return jax.shard_map(
        on_device,
        mesh=torus,
        in_specs=(
            P(GRP_SEQ, None),
            P(GRP_SEQ, None),
            P(),
            P(),
            P(),
            P(),
            P(None, SEQ),
            P(None, SEQ),
            P(GRP_SEQ),
            P(GRP_SEQ, None),
            P(GRP_SEQ),
            P(GRP, None),
            P(),
            P(GRP_SEQ, None),
            P(None, GRP_SEQ),
        ),
        out_specs=P(GRP_SEQ, None),
        check_vma=False,
    )
```

profile of v0, /device:TPU:32, one launch (start us, length us, event | category | flops | bytes accessed | tf_op | source)
XLA Modules:
  0.0 800.0 jit_solution(2683029863450592169)
XLA Ops:
  7.5 12.8 %all-gather.4 = bf16[128,768]{1,0:T(8,128)(2,1)S(1)} all-gather(bf16[32,768]{1,0:T(8,128)(2,1)S(1)} %split.19), channel_id=6, replica_groups=mesh['grp_0'=2,'grp_1'=2,'seq_0'=2,'seq_1'=4,'seq_2'=4] {'seq_2'}, dimensions={0}, use_global_device_ids=true | all-gather | bytes 245760 | tf_op jit(solution)/shard_map/all_gather | solution.py:27
  20.3 14.9 %all_gather.107 = bf16[16,32,768]{2,1,0:T(8,128)(2,1)} all-gather(bf16[4,32,768]{2,1,0:T(8,128)(2,1)S(1)} %bitcast.122), channel_id=1, replica_groups=mesh['grp_0'=2,'grp_1'=2,'seq_0'=2,'seq_1'=4,'seq_2'=4] {'seq_1'}, dimensions={0}, use_global_device_ids=true | all-gather | bytes 983040 | tf_op jit(solution)/shard_map/all_gather | solution.py:27
  36.4 5.8 convolution_convert_fusion.2
  57.4 9.6 %all-gather.28.cloned.1.call-done = bf16[32,32,768]{2,1,0:T(8,128)(2,1)} async-done(((bf16[16,32,768]{2,1,0:T(8,128)(2,1)}), bf16[32,32,768]{2,1,0:T(8,128)(2,1)}) %all-gather.28.cloned.1.call-update) | async-done | bytes 1572880 | tf_op jit(solution)/shard_map/all_gather | solution.py:27
  71.5 12.3 %all_gather.87 = bf16[8,8,768]{2,1,0:T(8,128)(2,1)S(1)} all-gather(bf16[2,8,768]{2,1,0:T(8,128)(2,1)S(1)} %bitcast.127), channel_id=1, replica_groups=mesh['grp_0'=2,'grp_1'=2,'seq_0'=2,'seq_1'=4,'seq_2'=4] {'seq_2'}, dimensions={0}, use_global_device_ids=true | all-gather | bytes 122880 | tf_op jit(solution)/shard_map/all_gather | solution.py:27
  83.9 13.2 %all_gather.88 = bf16[32,8,768]{2,1,0:T(8,128)(2,1)S(1)} all-gather(bf16[8,8,768]{2,1,0:T(8,128)(2,1)S(1)} %all_gather.87), channel_id=1, replica_groups=mesh['grp_0'=2,'grp_1'=2,'seq_0'=2,'seq_1'=4,'seq_2'=4] {'seq_1'}, dimensions={0}, use_global_device_ids=true | all-gather | bytes 491520 | tf_op jit(solution)/shard_map/all_gather | solution.py:27
  97.0 14.7 %all_gather.89 = bf16[64,8,768]{2,1,0:T(8,128)(2,1)} all-gather(bf16[32,8,768]{2,1,0:T(8,128)(2,1)S(1)} %all_gather.88), channel_id=1, replica_groups=mesh['grp_0'=2,'grp_1'=2,'seq_0'=2,'seq_1'=4,'seq_2'=4] {'seq_0'}, dimensions={0}, use_global_device_ids=true | all-gather | bytes 1179648 | tf_op jit(solution)/shard_map/all_gather | solution.py:27
  113.6 4.5 all_gather.92
  118.1 12.7 %all_gather.93 = bf16[16,8,768]{2,1,0:T(8,128)(2,1)S(1)} all-gather(bf16[4,8,768]{2,1,0:T(8,128)(2,1)S(1)} %all_gather.92), channel_id=1, replica_groups=mesh['grp_0'=2,'grp_1'=2,'seq_0'=2,'seq_1'=4,'seq_2'=4] {'seq_2'}, dimensions={0}, use_global_device_ids=true | all-gather | bytes 245760 | tf_op jit(solution)/shard_map/all_gather | solution.py:27
  130.8 15.6 %all_gather.94 = bf16[64,8,768]{2,1,0:T(8,128)(2,1)} all-gather(bf16[16,8,768]{2,1,0:T(8,128)(2,1)S(1)} %all_gather.93), channel_id=1, replica_groups=mesh['grp_0'=2,'grp_1'=2,'seq_0'=2,'seq_1'=4,'seq_2'=4] {'seq_1'}, dimensions={0}, use_global_device_ids=true | all-gather | bytes 983040 | tf_op jit(solution)/shard_map/all_gather | solution.py:27
  146.4 10.5 %all-gather.16.cloned.1.call-done = bf16[512,5120]{1,0:T(8,128)(2,1)} async-done(((bf16[16,5120]{1,0:T(8,128)(2,1)}), bf16[512,5120]{1,0:T(8,128)(2,1)}) %all-gather.16.cloned.1.call-update) | async-done | bytes 5242896 | tf_op jit(solution)/shard_map/all_gather | solution.py:143
  157.0 5.7 fusion.54
  162.7 5.9 all-gather.2
  170.5 4.8 all_gather.98
  175.2 13.7 %all_gather.99 = bf16[32,8,768]{2,1,0:T(8,128)(2,1)} all-gather(bf16[8,8,768]{2,1,0:T(8,128)(2,1)S(1)} %all_gather.98), channel_id=1, replica_groups=mesh['grp_0'=2,'grp_1'=2,'seq_0'=2,'seq_1'=4,'seq_2'=4] {'seq_2'}, dimensions={0}, use_global_device_ids=true | all-gather | bytes 491520 | tf_op jit(solution)/shard_map/all_gather | solution.py:27
  189.0 12.1 %all-gather.3 = bf16[32,768]{1,0:T(8,128)(2,1)S(1)} all-gather(bf16[8,768]{1,0:T(8,128)(2,1)S(1)} %get-tuple-element.197), channel_id=5, replica_groups=mesh['grp_0'=2,'grp_1'=2,'seq_0'=2,'seq_1'=4,'seq_2'=4] {'seq_1'}, dimensions={0}, use_global_device_ids=true | all-gather | bytes 61440 | tf_op jit(solution)/shard_map/all_gather | solution.py:27
  201.1 7.3 all_gather.102
  210.3 12.4 %all_gather.104 = bf16[32,8,768]{2,1,0:T(8,128)(2,1)} all-gather(bf16[16,8,768]{2,1,0:T(8,128)(2,1)S(1)} %all_gather.103), channel_id=1, replica_groups=mesh['grp_0'=2,'grp_1'=2,'seq_0'=2,'seq_1'=4,'seq_2'=4] {'grp_0'}, dimensions={0}, use_global_device_ids=true | all-gather | bytes 589824 | tf_op jit(solution)/shard_map/all_gather | solution.py:27
  230.1 84.2 %all-gather.18.cloned.1.call-done = bf16[512,5120]{0,1:T(8,128)(2,1)} async-done(((bf16[512,160]{0,1:T(8,128)(2,1)}), bf16[512,5120]{0,1:T(8,128)(2,1)}) %all-gather.18.cloned.1.call-update) | async-done | bytes 5242896 | tf_op jit(solution)/shard_map/all_gather | solution.py:150
  314.3 4.7 convolution_convert_fusion.3
  319.1 6.3 all-to-all-start
  329.4 13.0 %all-gather.24.cloned.1.call-done = bf16[128,8,768]{2,1,0:T(8,128)(2,1)} async-done(((bf16[32,8,768]{2,1,0:T(8,128)(2,1)}), bf16[128,8,768]{2,1,0:T(8,128)(2,1)}) %all-gather.24.cloned.1.call-update) | async-done | bytes 1572880 | tf_op jit(solution)/shard_map/all_gather | solution.py:27
  344.0 27.5 %all-gather.26.cloned.1.call-done = bf16[128,8,768]{2,1,0:T(8,128)(2,1)} async-done(((bf16[32,8,768]{2,1,0:T(8,128)(2,1)}), bf16[128,8,768]{2,1,0:T(8,128)(2,1)}) %all-gather.26.cloned.1.call-update) | async-done | bytes 1572880 | tf_op jit(solution)/shard_map/all_gather | solution.py:27
  379.7 8.8 %all-to-all-start.1 = ((bf16[32,2,4096]{2,1,0:T(2,128)(2,1)}), bf16[32,2,4096]{2,1,0:T(2,128)(2,1)}, u32[]{:S(2)}, u32[]{:S(2)}) async-start(bf16[32,2,4096]{2,1,0:T(2,128)(2,1)} %reshape.417), calls=%async_computation.1 | async-start | bytes 1048576 | tf_op jit(solution)/shard_map/all_to_all | solution.py:166
  391.2 70.6 %all-gather.32.cloned.1.call-done = bf16[128,32,768]{2,1,0:T(8,128)(2,1)} async-done(((bf16[64,32,768]{2,1,0:T(8,128)(2,1)}), bf16[128,32,768]{2,1,0:T(8,128)(2,1)}) %all-gather.32.cloned.1.call-update) | async-done | bytes 6291472 | tf_op jit(solution)/shard_map/all_gather | solution.py:27
  461.8 6.0 constant_dynamic-update-slice_fusion.2
  471.4 4.5 fusion.32
  476.0 8.1 %fusion.39 = bf16[256,768]{1,0:T(8,128)(2,1)S(1)} fusion(bf16[8192,768]{1,0:T(8,128)(2,1)} %bitcast.25, bf16[256,8192]{1,0:T(8,128)(2,1)S(1)} %get-tuple-element.206, f32[8192]{0:T(1024)S(1)} %copy-done.12, f32[256]{0:T(256)S(1)} %add_rsqrt_fusion), kind=kOutput, calls=%fused_computation.40 | convolution fusion | flops 3229810688 | bytes 17204224 | tf_op jit(solution)/shard_map/dot_general | solution.py:175
  484.4 148.8 %while.20 = (s32[]{:T(128)}, bf16[256,256]{1,0:T(8,128)(2,1)S(1)}, bf16[4352,256]{1,0:T(8,128)(2,1)S(1)}, s32[]{:T(128)}, s32[]{:T(128)}, /*index=5*/s32[]{:T(128)}, s32[]{:T(128)}, s32[]{:T(128)}) while((s32[]{:T(128)}, bf16[256,256]{1,0:T(8,128)(2,1)S(1)}, bf16[4352,256]{1,0:T(8,128)(2,1)S(1)}, s32[]{:T(128)}, s32[]{:T(128)}, ...), condition=%wide.region_9.10_spmd, body=%wide.region_8.9_spmd.sunk | while | flops 7 | bytes 1048763 | solution.py:200
  487.8 6.1 collective-permute-done
  495.9 7.1 collective-permute-done
  504.9 7.1 collective-permute-done
  514.1 7.1 collective-permute-done
  523.2 7.1 collective-permute-done
  532.2 7.1 collective-permute-done
  541.4 8.3 %collective-permute-done = bf16[256,256]{1,0:T(8,128)(2,1)S(1)} collective-permute-done((bf16[256,256]{1,0:T(8,128)(2,1)S(1)}, bf16[256,256]{1,0:T(8,128)(2,1)S(1)}, u32[]{:S(2)}, u32[]{:S(2)}) %collective-permute-start) | collective-permute-done | bytes 131104 | tf_op jit(solution)/shard_map/while/body/eval_jaxpr/ppermute | solution.py:53
  551.6 7.7 collective-permute-done
  561.3 7.0 collective-permute-done
  570.3 7.1 collective-permute-done
  579.4 7.1 collective-permute-done
  588.5 7.1 collective-permute-done
  597.6 7.1 collective-permute-done
  606.7 8.2 %collective-permute-done = bf16[256,256]{1,0:T(8,128)(2,1)S(1)} collective-permute-done((bf16[256,256]{1,0:T(8,128)(2,1)S(1)}, bf16[256,256]{1,0:T(8,128)(2,1)S(1)}, u32[]{:S(2)}, u32[]{:S(2)}) %collective-permute-start) | collective-permute-done | bytes 131104 | tf_op jit(solution)/shard_map/while/body/eval_jaxpr/ppermute | solution.py:53
  616.9 7.1 collective-permute-done
  626.0 7.1 collective-permute-done
  633.2 13.0 %while.21 = (s32[]{:T(128)}, bf16[4,256,128]{1,2,0:T(8,128)(2,1)S(1)}, s32[256]{0:T(256)S(1)}, bf16[4,256,128]{2,1,0:T(8,128)(2,1)S(1)}, bf16[4352,256]{1,0:T(8,...) while((s32[]{:T(128)}, bf16[4,256,128]{1,2,0:T(8,128)(2,1)S(1)}, s32[256]{0:T(256)S(1)}, ...), condition=%wide.region_13.14_spmd.clone, body=%wide.region_10.13_spmd.clone.sunk | while | flops 581636096 | bytes 16036973 | solution.py:215
  646.2 137.8 %all-gather.34.cloned.1.call-done = bf16[512,8192]{0,1:T(8,128)(2,1)} async-done(((bf16[512,64]{0,1:T(8,128)(2,1)}), bf16[512,8192]{0,1:T(8,128)(2,1)}) %all-gather.34.cloned.1.call-update) | async-done | bytes 8388624 | tf_op jit(solution)/shard_map/all_gather | solution.py:218
  784.0 9.1 %fusion.29 = bf16[256,8192]{1,0:T(8,128)(2,1)} fusion(bf16[256,512]{0,1:T(8,128)(2,1)S(1)} %bitcast.123, bf16[512,8192]{0,1:T(8,128)(2,1)} %all-gather.34.cloned.1.call-done, bf16[256,8192]{1,0:T(8,128)(2,1)} %copy-done.4), kind=kOutput, calls=%fused_computation.27 | convolution fusion | flops 2153775104 | bytes 17039360 | tf_op jit(solution)/shard_map/dot_general | solution.py:216
  (179 shorter events, 100.6 us)
Async XLA Ops:
  6.5 48.1 %copy-start = (bf16[1280,1280]{1,0:T(8,128)(2,1)S(1)}, bf16[1280,1280]{1,0:T(8,128)(2,1)}, u32[]{:S(2)}) copy-start(bf16[1280,1280]{1,0:T(8,128)(2,1)} %param.23) | copy-start | bytes 9830404
  6.5 60.5 %all-gather.28.cloned.1.call-start = ((), (), s32[]{:S(2)}) async-start(), calls=%async_computation.8 | async-start | bytes 2359296 | tf_op jit(solution)/shard_map/all_gather | solution.py:27
  35.2 121.7 %all-gather.16.cloned.1.call-start = ((), (), s32[]{:S(2)}) async-start(), calls=%async_computation.2 | async-start | bytes 5406720 | tf_op jit(solution)/shard_map/all_gather | solution.py:143
  36.4 12.7 %copy-start.9 = (s32[1,64]{1,0:T(1,128)S(1)}, s32[1,64]{1,0:T(1,128)}, u32[]{:S(2)}) copy-start(s32[1,64]{1,0:T(1,128)} %param.20) | copy-start | bytes 772
  42.2 12.5 %copy-start.5 = (bf16[64,1280]{1,0:T(8,128)(2,1)S(1)}, bf16[64,1280]{1,0:T(8,128)(2,1)}, u32[]{:S(2)}) copy-start(bf16[64,1280]{1,0:T(8,128)(2,1)} %param.19) | copy-start | bytes 491524
  49.1 7.3 copy-start.8
  50.6 16.5 %copy-start.7 = (bf16[64,768]{1,0:T(8,128)(2,1)S(1)}, bf16[64,768]{1,0:T(8,128)(2,1)}, u32[]{:S(2)}) copy-start(bf16[64,768]{1,0:T(8,128)(2,1)} %param.32) | copy-start | bytes 294916
  56.4 100.5 %copy-start.11 = (bf16[5120,160]{0,1:T(8,128)(2,1)S(1)}, bf16[5120,160]{0,1:T(8,128)(2,1)}, u32[]{:S(2)}) copy-start(bf16[5120,160]{0,1:T(8,128)(2,1)} %param.25) | copy-start | bytes 4915204
  57.3 165.5 %all-gather.30.cloned.1.call-start = ((), (), s32[]{:S(2)}) async-start(), calls=%async_computation.9 | async-start | bytes 4718592 | tf_op jit(solution)/shard_map/all_gather | solution.py:27
  67.1 157.5 %all-gather.20.cloned.1.call-start = ((), (), s32[]{:S(2)}) async-start(), calls=%async_computation.4 | async-start | bytes 2359296 | tf_op jit(solution)/shard_map/all_gather | solution.py:27
  111.8 115.6 %all-gather.22.cloned.1.call-start = ((), (), s32[]{:S(2)}) async-start(), calls=%async_computation.5 | async-start | bytes 2359296 | tf_op jit(solution)/shard_map/all_gather | solution.py:27
  146.4 167.9 %all-gather.18.cloned.1.call-start = ((), (), s32[]{:S(2)}) async-start(), calls=%async_computation.3 | async-start | bytes 5406720 | tf_op jit(solution)/shard_map/all_gather | solution.py:150
  162.6 61.5 %copy-start.14 = (s32[1,4]{1,0:T(1,128)S(1)}, s32[1,4]{1,0:T(1,128)}, u32[]{:S(2)}) copy-start(s32[1,4]{1,0:T(1,128)} %param.30) | copy-start | bytes 52
  162.6 61.6 %copy-start.10 = (s32[16]{0:T(128)S(1)}, s32[16]{0:T(128)}, u32[]{:S(2)}) copy-start(s32[16]{0:T(128)} %param.27) | copy-start | bytes 196
  162.6 61.9 %copy-start.13 = (s32[256]{0:T(256)S(1)}, s32[256]{0:T(256)}, u32[]{:S(2)}) copy-start(s32[256]{0:T(256)} %param.29) | copy-start | bytes 3076
  162.7 179.8 %all-gather.24.cloned.1.call-start = ((), (), s32[]{:S(2)}) async-start(), calls=%async_computation.6 | async-start | bytes 1966080 | tf_op jit(solution)/shard_map/all_gather | solution.py:27
  188.9 182.6 %all-gather.26.cloned.1.call-start = ((), (), s32[]{:S(2)}) async-start(), calls=%async_computation.7 | async-start | bytes 1966080 | tf_op jit(solution)/shard_map/all_gather | solution.py:27
  222.8 239.0 %all-gather.32.cloned.1.call-start = ((), (), s32[]{:S(2)}) async-start(), calls=%async_computation.10 | async-start | bytes 9437184 | tf_op jit(solution)/shard_map/all_gather | solution.py:27
  222.9 91.5 %copy-start.2 = (bf16[5120,256]{1,0:T(8,128)(2,1)S(1)}, bf16[5120,256]{1,0:T(8,128)(2,1)}, u32[]{:S(2)}) copy-start(bf16[5120,256]{1,0:T(8,128)(2,1)} %param.26) | copy-start | bytes 7864324
  223.5 560.5 %all-gather.34.cloned.1.call-start = ((), (), s32[]{:S(2)}) async-start(), calls=%async_computation.11 | async-start | bytes 8454144 | tf_op jit(solution)/shard_map/all_gather | solution.py:218
  319.1 9.0 %copy-start.3 = (bf16[2,2,2,4,4,8,768]{6,5,4,3,2,1,0:T(8,128)(2,1)S(1)}, bf16[2,2,2,4,4,8,768]{6,5,4,3,2,1,0:T(8,128)(2,1)}, u32[]{:S(2)}) copy-start(bf16[2,2,2,4,4,8,768]{6,5,4,3,2,1,0:T(8,128)(2,1)} %copy.71) | copy-start | bytes 4718596
  319.1 54.1 %all-to-all-start = ((bf16[32,16,256]{2,1,0:T(8,128)(2,1)}), bf16[32,16,256]{2,1,0:T(8,128)(2,1)S(1)}, u32[]{:S(2)}, u32[]{:S(2)}) async-start(bf16[32,16,256]{2,1,0:T(8,128)(2,1)} %bitcast.4), calls=%async_computation | async-start | bytes 524288 | tf_op jit(solution)/shard_map/all_to_all | solution.py:158
  379.7 88.1 %all-to-all-start.1 = ((bf16[32,2,4096]{2,1,0:T(2,128)(2,1)}), bf16[32,2,4096]{2,1,0:T(2,128)(2,1)}, u32[]{:S(2)}, u32[]{:S(2)}) async-start(bf16[32,2,4096]{2,1,0:T(2,128)(2,1)} %reshape.417), calls=%async_computation.1 | async-start | bytes 1048576 | tf_op jit(solution)/shard_map/all_to_all | solution.py:166
  471.4 4.5 copy-start.12
  475.9 8.2 %copy-start.4 = (bf16[256,8192]{1,0:T(8,128)(2,1)}, bf16[256,8192]{1,0:T(8,128)(2,1)S(1)}, u32[]{:S(2)}) copy-start(bf16[256,8192]{1,0:T(8,128)(2,1)S(1)} %get-tuple-element.206) | copy-start | bytes 12582916
  484.1 149.0 %copy-start.6 = (bf16[4,256,128]{1,2,0:T(8,128)(2,1)S(1)}, bf16[4,256,128]{1,2,0:T(8,128)(2,1)}, u32[]{:S(2)}) copy-start(bf16[4,256,128]{1,2,0:T(8,128)(2,1)} %custom-call.1) | copy-start | bytes 786436
  484.4 9.5 %collective-permute-start = (bf16[256,256]{1,0:T(8,128)(2,1)S(1)}, bf16[256,256]{1,0:T(8,128)(2,1)S(1)}, u32[]{:S(2)}, u32[]{:S(2)}) collective-permute-start(bf16[256,256]{1,0:T(8,128)(2,1)S(1)} %get-tuple-element.282), channel_id=1, source_target_pairs={{0,1},{1,2},{2,3},{3,4},{4,5},{5,6},{6,7},{7,8},{8,9},{9,10},{10,1... | collective-permute-start | bytes 393224 | tf_op jit(solution)/shard_map/while/body/eval_jaxpr/ppermute | solution.py:53
  493.9 9.0 %collective-permute-start = (bf16[256,256]{1,0:T(8,128)(2,1)S(1)}, bf16[256,256]{1,0:T(8,128)(2,1)S(1)}, u32[]{:S(2)}, u32[]{:S(2)}) collective-permute-start(bf16[256,256]{1,0:T(8,128)(2,1)S(1)} %get-tuple-element.282), channel_id=1, source_target_pairs={{0,1},{1,2},{2,3},{3,4},{4,5},{5,6},{6,7},{7,8},{8,9},{9,10},{10,1... | collective-permute-start | bytes 393224 | tf_op jit(solution)/shard_map/while/body/eval_jaxpr/ppermute | solution.py:53
  503.0 9.1 %collective-permute-start = (bf16[256,256]{1,0:T(8,128)(2,1)S(1)}, bf16[256,256]{1,0:T(8,128)(2,1)S(1)}, u32[]{:S(2)}, u32[]{:S(2)}) collective-permute-start(bf16[256,256]{1,0:T(8,128)(2,1)S(1)} %get-tuple-element.282), channel_id=1, source_target_pairs={{0,1},{1,2},{2,3},{3,4},{4,5},{5,6},{6,7},{7,8},{8,9},{9,10},{10,1... | collective-permute-start | bytes 393224 | tf_op jit(solution)/shard_map/while/body/eval_jaxpr/ppermute | solution.py:53
  512.1 9.1 %collective-permute-start = (bf16[256,256]{1,0:T(8,128)(2,1)S(1)}, bf16[256,256]{1,0:T(8,128)(2,1)S(1)}, u32[]{:S(2)}, u32[]{:S(2)}) collective-permute-start(bf16[256,256]{1,0:T(8,128)(2,1)S(1)} %get-tuple-element.282), channel_id=1, source_target_pairs={{0,1},{1,2},{2,3},{3,4},{4,5},{5,6},{6,7},{7,8},{8,9},{9,10},{10,1... | collective-permute-start | bytes 393224 | tf_op jit(solution)/shard_map/while/body/eval_jaxpr/ppermute | solution.py:53
  521.2 9.0 %collective-permute-start = (bf16[256,256]{1,0:T(8,128)(2,1)S(1)}, bf16[256,256]{1,0:T(8,128)(2,1)S(1)}, u32[]{:S(2)}, u32[]{:S(2)}) collective-permute-start(bf16[256,256]{1,0:T(8,128)(2,1)S(1)} %get-tuple-element.282), channel_id=1, source_target_pairs={{0,1},{1,2},{2,3},{3,4},{4,5},{5,6},{6,7},{7,8},{8,9},{9,10},{10,1... | collective-permute-start | bytes 393224 | tf_op jit(solution)/shard_map/while/body/eval_jaxpr/ppermute | solution.py:53
  530.3 9.1 %collective-permute-start = (bf16[256,256]{1,0:T(8,128)(2,1)S(1)}, bf16[256,256]{1,0:T(8,128)(2,1)S(1)}, u32[]{:S(2)}, u32[]{:S(2)}) collective-permute-start(bf16[256,256]{1,0:T(8,128)(2,1)S(1)} %get-tuple-element.282), channel_id=1, source_target_pairs={{0,1},{1,2},{2,3},{3,4},{4,5},{5,6},{6,7},{7,8},{8,9},{9,10},{10,1... | collective-permute-start | bytes 393224 | tf_op jit(solution)/shard_map/while/body/eval_jaxpr/ppermute | solution.py:53
  539.4 10.2 %collective-permute-start = (bf16[256,256]{1,0:T(8,128)(2,1)S(1)}, bf16[256,256]{1,0:T(8,128)(2,1)S(1)}, u32[]{:S(2)}, u32[]{:S(2)}) collective-permute-start(bf16[256,256]{1,0:T(8,128)(2,1)S(1)} %get-tuple-element.282), channel_id=1, source_target_pairs={{0,1},{1,2},{2,3},{3,4},{4,5},{5,6},{6,7},{7,8},{8,9},{9,10},{10,1... | collective-permute-start | bytes 393224 | tf_op jit(solution)/shard_map/while/body/eval_jaxpr/ppermute | solution.py:53
  549.7 9.6 %collective-permute-start = (bf16[256,256]{1,0:T(8,128)(2,1)S(1)}, bf16[256,256]{1,0:T(8,128)(2,1)S(1)}, u32[]{:S(2)}, u32[]{:S(2)}) collective-permute-start(bf16[256,256]{1,0:T(8,128)(2,1)S(1)} %get-tuple-element.282), channel_id=1, source_target_pairs={{0,1},{1,2},{2,3},{3,4},{4,5},{5,6},{6,7},{7,8},{8,9},{9,10},{10,1... | collective-permute-start | bytes 393224 | tf_op jit(solution)/shard_map/while/body/eval_jaxpr/ppermute | solution.py:53
  559.3 9.0 %collective-permute-start = (bf16[256,256]{1,0:T(8,128)(2,1)S(1)}, bf16[256,256]{1,0:T(8,128)(2,1)S(1)}, u32[]{:S(2)}, u32[]{:S(2)}) collective-permute-start(bf16[256,256]{1,0:T(8,128)(2,1)S(1)} %get-tuple-element.282), channel_id=1, source_target_pairs={{0,1},{1,2},{2,3},{3,4},{4,5},{5,6},{6,7},{7,8},{8,9},{9,10},{10,1... | collective-permute-start | bytes 393224 | tf_op jit(solution)/shard_map/while/body/eval_jaxpr/ppermute | solution.py:53
  568.4 9.1 %collective-permute-start = (bf16[256,256]{1,0:T(8,128)(2,1)S(1)}, bf16[256,256]{1,0:T(8,128)(2,1)S(1)}, u32[]{:S(2)}, u32[]{:S(2)}) collective-permute-start(bf16[256,256]{1,0:T(8,128)(2,1)S(1)} %get-tuple-element.282), channel_id=1, source_target_pairs={{0,1},{1,2},{2,3},{3,4},{4,5},{5,6},{6,7},{7,8},{8,9},{9,10},{10,1... | collective-permute-start | bytes 393224 | tf_op jit(solution)/shard_map/while/body/eval_jaxpr/ppermute | solution.py:53
  577.5 9.1 %collective-permute-start = (bf16[256,256]{1,0:T(8,128)(2,1)S(1)}, bf16[256,256]{1,0:T(8,128)(2,1)S(1)}, u32[]{:S(2)}, u32[]{:S(2)}) collective-permute-start(bf16[256,256]{1,0:T(8,128)(2,1)S(1)} %get-tuple-element.282), channel_id=1, source_target_pairs={{0,1},{1,2},{2,3},{3,4},{4,5},{5,6},{6,7},{7,8},{8,9},{9,10},{10,1... | collective-permute-start | bytes 393224 | tf_op jit(solution)/shard_map/while/body/eval_jaxpr/ppermute | solution.py:53
  586.6 9.0 %collective-permute-start = (bf16[256,256]{1,0:T(8,128)(2,1)S(1)}, bf16[256,256]{1,0:T(8,128)(2,1)S(1)}, u32[]{:S(2)}, u32[]{:S(2)}) collective-permute-start(bf16[256,256]{1,0:T(8,128)(2,1)S(1)} %get-tuple-element.282), channel_id=1, source_target_pairs={{0,1},{1,2},{2,3},{3,4},{4,5},{5,6},{6,7},{7,8},{8,9},{9,10},{10,1... | collective-permute-start | bytes 393224 | tf_op jit(solution)/shard_map/while/body/eval_jaxpr/ppermute | solution.py:53
  595.6 9.1 %collective-permute-start = (bf16[256,256]{1,0:T(8,128)(2,1)S(1)}, bf16[256,256]{1,0:T(8,128)(2,1)S(1)}, u32[]{:S(2)}, u32[]{:S(2)}) collective-permute-start(bf16[256,256]{1,0:T(8,128)(2,1)S(1)} %get-tuple-element.282), channel_id=1, source_target_pairs={{0,1},{1,2},{2,3},{3,4},{4,5},{5,6},{6,7},{7,8},{8,9},{9,10},{10,1... | collective-permute-start | bytes 393224 | tf_op jit(solution)/shard_map/while/body/eval_jaxpr/ppermute | solution.py:53
  604.8 10.1 %collective-permute-start = (bf16[256,256]{1,0:T(8,128)(2,1)S(1)}, bf16[256,256]{1,0:T(8,128)(2,1)S(1)}, u32[]{:S(2)}, u32[]{:S(2)}) collective-permute-start(bf16[256,256]{1,0:T(8,128)(2,1)S(1)} %get-tuple-element.282), channel_id=1, source_target_pairs={{0,1},{1,2},{2,3},{3,4},{4,5},{5,6},{6,7},{7,8},{8,9},{9,10},{10,1... | collective-permute-start | bytes 393224 | tf_op jit(solution)/shard_map/while/body/eval_jaxpr/ppermute | solution.py:53
  614.9 9.1 %collective-permute-start = (bf16[256,256]{1,0:T(8,128)(2,1)S(1)}, bf16[256,256]{1,0:T(8,128)(2,1)S(1)}, u32[]{:S(2)}, u32[]{:S(2)}) collective-permute-start(bf16[256,256]{1,0:T(8,128)(2,1)S(1)} %get-tuple-element.282), channel_id=1, source_target_pairs={{0,1},{1,2},{2,3},{3,4},{4,5},{5,6},{6,7},{7,8},{8,9},{9,10},{10,1... | collective-permute-start | bytes 393224 | tf_op jit(solution)/shard_map/while/body/eval_jaxpr/ppermute | solution.py:53
  624.1 9.1 %collective-permute-start = (bf16[256,256]{1,0:T(8,128)(2,1)S(1)}, bf16[256,256]{1,0:T(8,128)(2,1)S(1)}, u32[]{:S(2)}, u32[]{:S(2)}) collective-permute-start(bf16[256,256]{1,0:T(8,128)(2,1)S(1)} %get-tuple-element.282), channel_id=1, source_target_pairs={{0,1},{1,2},{2,3},{3,4},{4,5},{5,6},{6,7},{7,8},{8,9},{9,10},{10,1... | collective-permute-start | bytes 393224 | tf_op jit(solution)/shard_map/while/body/eval_jaxpr/ppermute | solution.py:53
  784.0 9.2 %copy-start.1 = (bf16[1280,1280]{1,0:T(8,128)(2,1)S(1)}, bf16[1280,1280]{1,0:T(8,128)(2,1)}, u32[]{:S(2)}) copy-start(bf16[1280,1280]{1,0:T(8,128)(2,1)} %param.23) | copy-start | bytes 9830404
Sparse Core Ops, SparseCore 0:
  35.4 31.6 all-gather.27
  70.1 86.8 all-gather.15
  158.6 13.0 all-gather.29
  173.2 13.7 all-gather.19
  188.5 37.2 all-gather.21
  228.7 85.5 all-gather.17
  316.0 26.3 all-gather.23
  344.1 27.4 all-gather.25
  373.2 88.5 all-gather.31
  463.3 320.6 all-gather.33
where the time goes:
time: 802 us; the launch traced here: 800 us
  waiting for transfers between devices  470 us (59%)
  blocking collectives  167 us (21%)
  matrix products  52.8 us (7%)
  starting transfers between devices  47.6 us (6%)
  local copies, waits for them, and re-layouts  40.3 us (5%)
  between operations  13.9 us (2%)
    all_gather x18, blocking collectives, all_blocks(): parts = lax.all_gather(parts, axes[k], axis=0, tiled=True)  167 us
    all_gather x1, waiting for transfers between devices, on_device(): lax.all_gather(attn_out, GRP_SEQ, axis=1, tiled=True)  138 us
    all_gather x7, waiting for transfers between devices, all_blocks(): parts = lax.all_gather(parts, axes[k], axis=0, tiled=True)  121 us
    ppermute x16, waiting for transfers between devices, from_behind(): lax.ppermute(value, axis, [(source, source + steps) for source in range(f...  116 us
    all_gather x1, waiting for transfers between devices, on_device(): lax.all_gather(hidden_part, SEQ, axis=1, tiled=True)  84.2 us
    ppermute x16, starting transfers between devices, from_behind(): lax.ppermute(value, axis, [(source, source + steps) for source in range(f...  32.2 us
  transfers between devices with their start and end apart: 28, of which 23 were waited for; matrix products, arithmetic and copies ran while one was open for 11% of the time, Pallas kernels for 0%

commit v1 on v0

v1 whole, which is shorter than its diff:
```python
import jax
import jax.numpy as jnp
from jax import lax
from jax.experimental import pallas as pl
from jax.experimental.pallas import tpu as pltpu
from jax.sharding import Mesh
from jax.sharding import PartitionSpec as P

VHEADS = 16
XLO, CORE, XHI, Z, Y = ("grp_0", "grp_1", "seq_0", "seq_1", "seq_2")
SEQ = (XHI, Z, Y)
ZY = (Z, Y)
SAME_CORE = (XLO, XHI, Z, Y)
GRP_SEQ = (XLO, CORE, XHI, Z, Y)
GRP = (XLO, CORE)
EPSILON = 1e-06
NEG = -1e30
FAR = 1 << 30
BF = jnp.bfloat16
F32 = jnp.float32
MEM = 56 * 1024 * 1024


def dot_f32(a, b, ca=1, cb=0):
    return lax.dot_general(a, b, (((ca,), (cb,)), ((), ())), preferred_element_type=F32)


def window_kernel(x_ref, prow_ref, pcol_ref, gain_ref, w_ref, wo_ref, mgain_ref, o_ref, n_ref, p_ref):
    step = pl.program_id(0)
    rows, feats = x_ref.shape
    head = feats // VHEADS

    @pl.when(step == 0)
    def _():
        x = x_ref[...].astype(F32)
        mean = jnp.mean(x * x, axis=-1, keepdims=True)
        n_ref[...] = (x * lax.rsqrt(mean + EPSILON) * gain_ref[...]).astype(BF)

    for part in range(3):

        @pl.when(step == part)
        def _(part=part):
            p_ref[part] = dot_f32(n_ref[...], w_ref[...]).astype(BF)

    @pl.when(step == 2)
    def _():
        q, k, v = (p_ref[0], p_ref[1], p_ref[2])
        lane = lax.broadcasted_iota(jnp.int32, (rows, feats), 1)
        same = pcol_ref[...] == prow_ref[...]
        mixed = jnp.zeros((rows, feats), F32)
        for h in range(VHEADS):
            mine = (lane >= h * head) & (lane < (h + 1) * head)
            s = dot_f32(jnp.where(mine, q, jnp.zeros_like(q)), k, 1, 1) * head ** (-0.5)
            s = jnp.where(same, s, NEG)
            w = jnp.exp(s - jnp.max(s, axis=-1, keepdims=True))
            total = jnp.sum(w, axis=-1, keepdims=True)
            mixed = jnp.where(mine, dot_f32(w.astype(BF), v) / total, mixed)
        resid = x_ref[...].astype(F32) + dot_f32(mixed.astype(BF), wo_ref[...])
        mean = jnp.mean(resid * resid, axis=-1, keepdims=True)
        merged = (resid * lax.rsqrt(mean + EPSILON) * mgain_ref[...]).astype(BF)
        r_out = lax.broadcasted_iota(jnp.int32, (rows // 4, rows), 0)
        r_in = lax.broadcasted_iota(jnp.int32, (rows // 4, rows), 1)
        for j in range(4):
            pick = jnp.where(r_in == 4 * r_out + j, 1.0, 0.0).astype(BF)
            o_ref[:, j * feats : (j + 1) * feats] = dot_f32(pick, merged).astype(BF)


def window_layer(patches, piece_ids, vit_gain, vit_qkv, vit_out, merge_gain):
    rows, feats = patches.shape
    whole = lambda *shape: pl.BlockSpec(shape, lambda i: (0,) * len(shape))
    return pl.pallas_call(
        window_kernel,
        grid=(3,),
        in_specs=[
            whole(rows, feats),
            whole(1, rows),
            whole(rows, 1),
            whole(1, feats),
            pl.BlockSpec((feats, feats), lambda i: (0, i)),
            whole(feats, feats),
            whole(1, feats),
        ],
        out_specs=whole(rows // 4, 4 * feats),
        out_shape=jax.ShapeDtypeStruct((rows // 4, 4 * feats), BF),
        scratch_shapes=[pltpu.VMEM((rows, feats), BF), pltpu.VMEM((3, rows, feats), BF)],
        compiler_params=pltpu.CompilerParams(vmem_limit_bytes=MEM),
        name="window_layer",
    )(
        patches,
        piece_ids.reshape(1, rows),
        piece_ids.reshape(rows, 1),
        vit_gain.reshape(1, feats),
        vit_qkv,
        vit_out,
        merge_gain.reshape(1, feats),
    )


def project_kernel(core_ref, x_ref, gain_ref, own_ref, oth_ref, o_ref, r_ref, acc_ref):
    step = pl.program_id(0)
    depth = own_ref.shape[1]
    core = core_ref[0]

    @pl.when(step == 0)
    def _():
        rows, width = x_ref.shape
        total = jnp.zeros((rows, 1), F32)
        for c in range(0, width, 1024):
            x = x_ref[:, c : c + 1024].astype(F32)
            total = total + jnp.sum(x * x, axis=-1, keepdims=True)
        r_ref[...] = lax.rsqrt(total / width + EPSILON)
        acc_ref[...] = jnp.zeros_like(acc_ref)

    def add(w_ref, which):
        start = pl.multiple_of(((step % 2) * 2 + which) * depth, depth)
        x = x_ref[:, pl.ds(start, depth)].astype(F32)
        n = (x * r_ref[...] * gain_ref[:, pl.ds(start, depth)]).astype(BF)
        acc_ref[...] += dot_f32(n, w_ref[0])

    @pl.when(step < 2)
    def _():
        add(own_ref, core)

    @pl.when(step >= 2)
    def _():
        add(oth_ref, 1 - core)

    @pl.when(step == 3)
    def _():
        o_ref[...] = acc_ref[...].astype(BF)


def project(core, x, gain, own, oth):
    rows, width = x.shape
    depth, cols = own.shape[1:]
    return pl.pallas_call(
        project_kernel,
        grid_spec=pltpu.PrefetchScalarGridSpec(
            num_scalar_prefetch=1,
            grid=(4,),
            in_specs=[
                pl.BlockSpec((rows, width), lambda i, c: (0, 0)),
                pl.BlockSpec((1, width), lambda i, c: (0, 0)),
                pl.BlockSpec((1, depth, cols), lambda i, c: (jnp.minimum(i, 1), 0, 0)),
                pl.BlockSpec((1, depth, cols), lambda i, c: (jnp.maximum(i - 2, 0), 0, 0)),
            ],
            out_specs=pl.BlockSpec((rows, cols), lambda i, c: (0, 0)),
            scratch_shapes=[pltpu.VMEM((rows, 1), F32), pltpu.VMEM((rows, cols), F32)],
        ),
        out_shape=jax.ShapeDtypeStruct((rows, cols), BF),
        compiler_params=pltpu.CompilerParams(vmem_limit_bytes=MEM),
        name="project",
    )(core, x, gain.reshape(1, width), own, oth)


def attention_kernel(
    own_ref, img_ref, kv_ref, kvi_ref, index_ref, qpos_ref, qstart_ref, kpos_ref, ownpos_ref, ipos_ref, iown_ref,
    o_ref, m_ref, l_ref, acc_ref,
):
    rows = own_ref.shape[0]
    slots = img_ref.shape[0]
    head = kv_ref.shape[2] // 2
    heads = o_ref.shape[1] // head
    width = heads * head
    blocks = kv_ref.shape[0]
    m_ref[...] = jnp.full_like(m_ref, NEG)
    l_ref[...] = jnp.zeros_like(l_ref)
    acc_ref[...] = jnp.zeros_like(acc_ref)
    index = index_ref[...]
    picker = (index == lax.broadcasted_iota(jnp.int32, (rows, slots), 1)).astype(F32).astype(BF)
    is_img = index < slots
    queries = [
        jnp.where(
            is_img,
            dot_f32(picker, img_ref[:, h * head : (h + 1) * head]),
            own_ref[:, h * head : (h + 1) * head].astype(F32),
        ).astype(BF)
        for h in range(heads)
    ]
    qpos, qstart = (qpos_ref[...], qstart_ref[...])
    scale = head ** (-0.5)

    def fold(keys, values, kpos):
        allowed = (kpos >= qstart) & (kpos <= qpos)
        for h in range(heads):
            s = jnp.where(allowed, dot_f32(queries[h], keys, 1, 1) * scale, NEG)
            old = m_ref[h]
            new = jnp.maximum(old, jnp.max(s, axis=-1, keepdims=True))
            shrink = jnp.exp(old - new)
            w = jnp.exp(s - new)
            l_ref[h] = l_ref[h] * shrink + jnp.sum(w, axis=-1, keepdims=True)
            acc_ref[h] = acc_ref[h] * shrink + dot_f32(w.astype(BF), values)
            m_ref[h] = new

    fold(own_ref[:, width : width + head], own_ref[:, width + head :], ownpos_ref[...])
    fold(img_ref[:, width : width + head], img_ref[:, width + head :], iown_ref[...])
    fold(kvi_ref[:, :head], kvi_ref[:, head:], ipos_ref[...])

    def step(i, carry):
        pair = kv_ref[pl.ds(2 * i, 2), :rows, :].reshape(2 * rows, 2 * head)
        fold(pair[:, :head], pair[:, head:], kpos_ref[i])
        return carry

    lax.fori_loop(0, blocks // 2, step, 0)
    for h in range(heads):
        o_ref[:, h * head : (h + 1) * head] = (acc_ref[h] / l_ref[h]).astype(BF)


def attention(own, img, kv, kvi, index, qpos, qstart, kpos, ownpos, ipos, iown):
    rows = own.shape[0]
    head = kv.shape[2] // 2
    heads = (own.shape[1] - 2 * head) // head
    return pl.pallas_call(
        attention_kernel,
        out_shape=jax.ShapeDtypeStruct((rows, heads * head), BF),
        scratch_shapes=[
            pltpu.VMEM((heads, rows, 1), F32),
            pltpu.VMEM((heads, rows, 1), F32),
            pltpu.VMEM((heads, rows, head), F32),
        ],
        compiler_params=pltpu.CompilerParams(vmem_limit_bytes=MEM),
        name="attention",
    )(own, img, kv, kvi, index, qpos, qstart, kpos, ownpos, ipos, iown)


def output_kernel(core_ref, att_ref, tok_ref, img_ref, index_ref, own_ref, oth_ref, o_ref):
    step = pl.program_id(0)
    rows = tok_ref.shape[0]
    slots = img_ref.shape[0]
    tiles = own_ref.shape[1]
    lanes = own_ref.shape[3]
    index = index_ref[...]
    picker = (index == lax.broadcasted_iota(jnp.int32, (rows, slots), 1)).astype(F32).astype(BF)
    is_img = index < slots

    def body(w_ref):
        for t in range(0, tiles, 2):
            at = slice(t * lanes, (t + 2) * lanes)
            w = jnp.concatenate([w_ref[0, t], w_ref[0, t + 1]], axis=1)
            update = dot_f32(att_ref[...], w)
            base = jnp.where(is_img, dot_f32(picker, img_ref[:, at]), tok_ref[:, at].astype(F32))
            o_ref[:, at] = (base + update).astype(BF)

    @pl.when(step < 4)
    def _():
        body(own_ref)

    @pl.when(step >= 4)
    def _():
        body(oth_ref)


def output_layer(core, att, tokens, images, index, own, oth):
    rows, width = tokens.shape
    slots = images.shape[0]
    tiles, depth, lanes = own.shape[1:]
    half = tiles // 2
    cols = half * lanes

    def column(i, c):
        side = jnp.where(i < 4, c[0], 1 - c[0])
        return (0, ((i // 2) % 2) * 4 + side * 2 + i % 2)

    return pl.pallas_call(
        output_kernel,
        grid_spec=pltpu.PrefetchScalarGridSpec(
            num_scalar_prefetch=1,
            grid=(8,),
            in_specs=[
                pl.BlockSpec(att.shape, lambda i, c: (0, 0)),
                pl.BlockSpec((rows, cols), column),
                pl.BlockSpec((slots, cols), column),
                pl.BlockSpec((rows, 1), lambda i, c: (0, 0)),
                pl.BlockSpec(
                    (1, half, depth, lanes),
                    lambda i, c: (jnp.minimum(i, 3) // 2, jnp.minimum(i, 3) % 2, 0, 0),
                ),
                pl.BlockSpec(
                    (1, half, depth, lanes),
                    lambda i, c: (jnp.maximum(i - 4, 0) // 2, jnp.maximum(i - 4, 0) % 2, 0, 0),
                ),
            ],
            out_specs=pl.BlockSpec((rows, cols), column),
        ),
        out_shape=jax.ShapeDtypeStruct((rows, width), BF),
        compiler_params=pltpu.CompilerParams(vmem_limit_bytes=MEM),
        name="output_layer",
    )(core, att, tokens, images, index, own, oth)


def swap(x, axis):
    return lax.ppermute(x, axis, [(0, 1), (1, 0)])


def turns(x, axis):
    count = lax.axis_size(axis)
    me = lax.axis_index(axis)
    yield me, x
    for k in range(1, count):
        yield (me - k) % count, lax.ppermute(x, axis, [(i, (i + k) % count) for i in range(count)])


def gather_zy(x, first):
    nz, ny = (lax.axis_size(Z), lax.axis_size(Y))
    if first == Z:
        line = jnp.zeros((nz, 1) + x.shape, x.dtype)
        for at, part in turns(x, Z):
            line = lax.dynamic_update_slice_in_dim(line, part[None, None], at, 0)
        plane = jnp.zeros((nz, ny) + x.shape, x.dtype)
        for at, part in turns(line, Y):
            plane = lax.dynamic_update_slice_in_dim(plane, part, at, 1)
    else:
        line = jnp.zeros((1, ny) + x.shape, x.dtype)
        for at, part in turns(x, Y):
            line = lax.dynamic_update_slice_in_dim(line, part[None, None], at, 1)
        plane = jnp.zeros((nz, ny) + x.shape, x.dtype)
        for at, part in turns(line, Z):
            plane = lax.dynamic_update_slice_in_dim(plane, part, at, 0)
    return plane


def copies_to(x, axes):
    count = lax.axis_size(axes)
    return lax.all_to_all(jnp.broadcast_to(x[None], (count,) + x.shape), axes, 0, 0, tiled=True)


def partner_halves(x, axis, core):
    size = x.shape[axis] // 2
    mine = swap(lax.dynamic_slice_in_dim(x, core * size, size, axis), XHI)
    other = swap(mine, CORE)
    buffer = jnp.zeros_like(x)
    buffer = lax.dynamic_update_slice_in_dim(buffer, mine, core * size, axis)
    return lax.dynamic_update_slice_in_dim(buffer, other, (1 - core) * size, axis)


def keys_for_later(block, x_hi, zy):
    below = lax.ppermute(block, XHI, [(0, 1)])
    count = lax.axis_size(ZY)
    receiver = jnp.arange(count, dtype=jnp.int32)
    take_below = ((x_hi == 1) & (receiver <= zy)).reshape((count,) + (1,) * block.ndim)
    outgoing = jnp.where(take_below, below[None], block[None])
    return lax.all_to_all(outgoing, ZY, 0, 0, tiled=True)


def on_device(
    patches, piece_ids, vit_gain, vit_qkv, vit_out, merge_gain, merge_up, merge_down, dest,
    tokens, image_index, doc_lengths, attn_gain, attn_qkv, attn_out,
):
    core = lax.axis_index(CORE)
    x_hi = lax.axis_index(XHI)
    zy = lax.axis_index(ZY)
    y_odd = lax.axis_index(Y) % 2
    seq_count = lax.axis_size(SEQ)
    seq_index = lax.axis_index(SEQ)
    places = seq_count // 2
    tok_rows, width = tokens.shape
    core_arg = core.reshape(1).astype(jnp.int32)

    qkv_own = copies_to(attn_qkv, SAME_CORE)
    qkv_own = qkv_own.reshape(2, -1, attn_qkv.shape[1])
    qkv_oth = swap(qkv_own, CORE)

    depth, sliver = attn_out.shape
    upper, lower = (attn_out[: depth // 2], attn_out[depth // 2 :])
    give = jnp.where(y_odd == 1, upper, lower)
    keep = jnp.where(y_odd == 1, lower, upper)
    got = lax.ppermute(give, Y, [(0, 1), (1, 0), (2, 3), (3, 2)])
    tile = jnp.where(
        y_odd == 1, jnp.concatenate([got, keep], axis=1), jnp.concatenate([keep, got], axis=1)
    )
    out_own = lax.all_gather(tile, SAME_CORE, axis=0, tiled=False)
    out_own = out_own.reshape(2, -1, depth, 2 * sliver)
    out_oth = swap(out_own, CORE)

    up_own = merge_up.T
    up_oth = partner_halves(up_own, 1, core)
    down_oth = partner_halves(merge_down, 0, core)

    merge_in = window_layer(patches, piece_ids, vit_gain, vit_qkv, vit_out, merge_gain)
    own_rows = merge_in.shape[0]
    half = merge_in.shape[1] // 2
    note = jnp.broadcast_to(dest.astype(BF)[:, None], (own_rows, 128))
    part_a = gather_zy(jnp.concatenate([merge_in[:, :half], note], axis=1), Z)
    part_b = gather_zy(merge_in[:, half:], Y)
    part_a = part_a.reshape(places * own_rows, half + 128)
    part_b = part_b.reshape(places * own_rows, half)
    targets = part_a[:, half].astype(jnp.int32)

    def hidden(weights):
        total = dot_f32(weights[:, :half], part_a[:, :half], 1, 1) + dot_f32(weights[:, half:], part_b, 1, 1)
        return jax.nn.gelu(total, approximate=False).astype(BF)

    mine, theirs = (hidden(up_own), hidden(up_oth))
    hidden_0 = gather_zy(jnp.where(x_hi == 0, mine, theirs), Z).reshape(-1, places * own_rows)
    hidden_1 = gather_zy(jnp.where(x_hi == 0, theirs, mine), Y).reshape(-1, places * own_rows)
    middle = hidden_0.shape[0]

    def columns(weights):
        return (
            dot_f32(hidden_0, weights[:middle], 0, 0) + dot_f32(hidden_1, weights[middle:], 0, 0)
        ).astype(BF)

    mine, theirs = (columns(merge_down), columns(down_oth))
    merged = jnp.concatenate(
        [jnp.where(x_hi == 0, mine, theirs), jnp.where(x_hi == 0, theirs, mine)], axis=1
    )

    receivers = jnp.arange(seq_count, dtype=jnp.int32)
    row_home = jnp.arange(places * own_rows, dtype=jnp.int32) // own_rows
    homes = jnp.arange(places, dtype=jnp.int32)
    select = (targets[None, None, :] == receivers[:, None, None]) & (
        row_home[None, None, :] == homes[None, :, None]
    )
    outgoing = dot_f32(select.astype(BF).reshape(seq_count * places, -1), merged).astype(BF)
    arrived = lax.all_to_all(
        outgoing.reshape(seq_count, places, -1), SEQ, split_axis=0, concat_axis=0, tiled=True
    )
    arrived = arrived.reshape(2, places, places, 2, -1)
    images = arrived.transpose(0, 2, 3, 1, 4).reshape(seq_count, width)

    proj_text = project(core_arg, tokens, attn_gain, qkv_own, qkv_oth)
    query_width = depth
    index_row = jnp.broadcast_to(image_index.astype(BF)[None, :], (16, tok_rows))
    block = jnp.concatenate([proj_text[:, query_width:], index_row], axis=0)
    kv_text = keys_for_later(block, x_hi, zy)

    proj_img = project(core_arg, images, attn_gain, qkv_own, qkv_oth)
    kv_img = keys_for_later(proj_img[:, query_width:], x_hi, zy)

    positions = seq_index * tok_rows + jnp.arange(tok_rows, dtype=jnp.int32)
    lengths = doc_lengths[0]
    order_of = jnp.arange(lengths.shape[0], dtype=jnp.int32)
    starts = jnp.sum(jnp.where(order_of[None, :] < order_of[:, None], lengths[None, :], 0), axis=1)
    doc_start = jnp.max(jnp.where(starts[None, :] <= positions[:, None], starts[None, :], 0), axis=1)
    slot_ids = jnp.arange(seq_count, dtype=jnp.int32)
    within = jnp.arange(tok_rows, dtype=jnp.int32)
    home = jnp.where(x_hi == 0, homes, jnp.where(homes >= zy, homes, homes + places))
    useful = (x_hi == 1) | (homes < zy)
    indexes = kv_text[:, tok_rows, :].astype(jnp.int32)
    kpos = jnp.where(
        (indexes == seq_count) & useful[:, None], home[:, None] * tok_rows + within[None, :], FAR
    )
    ownpos = jnp.where(image_index == seq_count, positions, FAR)
    hits = indexes[:, None, :] == slot_ids[None, :, None]
    ipos = jnp.min(
        jnp.where(hits & useful[:, None, None], (home[:, None] * tok_rows + within[None, :])[:, None, :], FAR),
        axis=-1,
    )
    iown = jnp.min(
        jnp.where(image_index[None, :] == slot_ids[:, None], positions[None, :], FAR), axis=-1
    )

    index_col = image_index.reshape(tok_rows, 1)
    attended = attention(
        proj_text,
        proj_img,
        kv_text,
        kv_img.reshape(-1, kv_img.shape[2]),
        index_col,
        positions.reshape(tok_rows, 1),
        doc_start.reshape(tok_rows, 1),
        kpos.reshape(places // 2, 1, 2 * tok_rows),
        ownpos.reshape(1, tok_rows),
        ipos.reshape(1, -1),
        iown.reshape(1, -1),
    )
    return output_layer(core_arg, attended, tokens, images, index_col, out_own, out_oth)


def solution(mesh):
    torus = Mesh(mesh.devices.reshape(2, 2, 2, 4, 4), GRP_SEQ)
    return jax.shard_map(
        on_device,
        mesh=torus,
        in_specs=(
            P(GRP_SEQ, None),
            P(GRP_SEQ, None),
            P(),
            P(),
            P(),
            P(),
            P(None, SEQ),
            P(None, SEQ),
            P(GRP_SEQ),
            P(GRP_SEQ, None),
            P(GRP_SEQ),
            P(GRP, None),
            P(),
            P(GRP_SEQ, None),
            P(None, GRP_SEQ),
        ),
        out_specs=P(GRP_SEQ, None),
        check_vma=False,
    )
```

time: 802 us -> 641 us (0.80); the launches traced: 800 us -> 629 us
  blocking collectives: 167 us -> 0 us
  waiting for transfers between devices: 470 us -> 387 us
  starting transfers between devices: 47.6 us -> 121 us
  Pallas kernels: 0 us -> 62.4 us
  matrix products: 52.8 us -> 9.26 us
  local copies, waits for them, and re-layouts: 40.3 us -> 26.9 us
    all_gather x18 -> x0, blocking collectives: 167 us -> none  [all_blocks(): parts = lax.all_gather(parts, axes[k], axis=0, tiled=True)]
    all_gather x10 -> x1, waiting for transfers between devices: 353 us -> 263 us  [on_device(): out_own = lax.all_gather(tile, SAME_CORE, axis=0, tiled=False)]
    pallas_call x0 -> x5, Pallas kernels: none -> 62.4 us  [the longest x1 22.8 us: attention(): pl.pallas_call(attention_kernel, out_shape=jax.ShapeDtypeStruct((rows, he...]
    ppermute x16 -> x33, starting transfers between devices: 32.2 us -> 81.6 us  [the longest x24 63.9 us: turns(): lax.ppermute(x, axis, [(i, (i + k) % count) for i in range(count)])]
    dot_general x18 -> x9, matrix products: 52.8 us -> 9.26 us  [dot_f32(): lax.dot_general(a, b, (((ca,), (cb,)), ((), ())), preferred_element_type=...]
    all_to_all x2 -> x4, starting transfers between devices: 15 us -> 39.5 us  [the longest x1 18.3 us: on_device(): lax.all_to_all(outgoing.reshape(seq_count, places, -1), SEQ, split_axis=0...]
    all_to_all x2 -> x4, waiting for transfers between devices: 0.01 us -> 15.2 us  [the longest x2 15.2 us: keys_for_later(): return lax.all_to_all(outgoing, ZY, 0, 0, tiled=True)]
    unnamed x36 -> x33, local copies, waits for them, and re-layouts: 12.7 us -> 1.4 us
  transfers between devices with their start and end apart: 28 -> 38, of which waited for: 23 -> 18; matrix products, arithmetic and copies ran while one was open for 11% -> 6% of each run, Pallas kernels for 0% -> 7%
where the time goes in v1:
time: 641 us; the launch traced here: 629 us
  waiting for transfers between devices  387 us (60%)
  starting transfers between devices  121 us (19%)
  Pallas kernels  62.4 us (10%)
  local copies, waits for them, and re-layouts  26.9 us (4%)
  between operations  14.3 us (2%)
  matrix products  9.26 us (1%)
  other arithmetic  8.24 us (1%)
    all_gather x1, waiting for transfers between devices, on_device(): out_own = lax.all_gather(tile, SAME_CORE, axis=0, tiled=False)  263 us
    ppermute x1, waiting for transfers between devices, on_device(): got = lax.ppermute(give, Y, [(0, 1), (1, 0), (2, 3), (3, 2)])  69 us
    ppermute x24, starting transfers between devices, turns(): lax.ppermute(x, axis, [(i, (i + k) % count) for i in range(count)])  63.9 us
    ppermute x24, waiting for transfers between devices, turns(): lax.ppermute(x, axis, [(i, (i + k) % count) for i in range(count)])  34.3 us
    pallas_call x1, Pallas kernels, attention(): pl.pallas_call(attention_kernel, out_shape=jax.ShapeDtypeStruct((rows, he...  22.8 us
    pallas_call x2, Pallas kernels, project(): pl.pallas_call(project_kernel, grid_spec=pltpu.PrefetchScalarGridSpec(num...  18.7 us
    all_to_all x1, starting transfers between devices, on_device(): lax.all_to_all(outgoing.reshape(seq_count, places, -1), SEQ, split_axis=0...  18.3 us
    all_to_all x2, waiting for transfers between devices, keys_for_later(): return lax.all_to_all(outgoing, ZY, 0, 0, tiled=True)  15.2 us
  transfers between devices with their start and end apart: 38, of which 18 were waited for; matrix products, arithmetic and copies ran while one was open for 6% of the time, Pallas kernels for 7%

profile of v1, /device:TPU:32, one launch (start us, length us, event | category | flops | bytes accessed | tf_op | source)
XLA Modules:
  0.0 629.0 jit_solution(12188609403446228627)
XLA Ops:
  10.5 9.7 %window_layer.1 = bf16[16,5120]{1,0:T(8,128)(2,1)} custom-call(bf16[64,1280]{1,0:T(8,128)(2,1)} %x_ref.3, s32[1,64]{1,0:T(1,128)} %prow_ref.1, s32[64,1]{1,0:T(8,128)} %copy.42.pcol_ref, f32[1,1280]{1,0:T(1,128)} %reshape.338.gain_ref, bf16[1280,3840]{1,0:T(8,128)(2,1)} %w_ref.1, bf16[1280,1280]{1,0:T(8,128)(2,1)} %wo_ref.1, f32[1,1280]{1,0:T(1,128)} %reshape.339.mgain_ref), custom_call_target="tpu_custom_call" | custom-call | tf_op jit(solution)/shard_map/window_layer/pallas_call | solution.py:71
  21.1 1.6 collective-permute-start.7
  22.7 2.9 collective-permute-start.8
  27.1 2.0 collective-permute-start.1
  29.1 3.4 broadcast_in_dim.219
  32.5 8.5 %all-to-all-start = ((bf16[64,64,768]{2,1,0:T(8,128)(2,1)}), bf16[64,64,768]{2,1,0:T(8,128)(2,1)}, u32[]{:S(2)}, u32[]{:S(2)}) async-start(bf16[64,64,768]{2,1,0:T(8,128)(2,1)} %broadcast_in_dim.219), calls=%async_computation | async-start | bytes 12582912 | tf_op jit(solution)/shard_map/all_to_all | solution.py:324
  42.0 1.5 collective-permute-start.31
  43.5 2.1 dynamic-slice_bitcast_fusion
  47.5 69.0 %collective-permute-done.31 = bf16[256,64]{1,0:T(8,128)(2,1)} collective-permute-done((bf16[256,64]{1,0:T(8,128)(2,1)}, bf16[256,64]{1,0:T(8,128)(2,1)}, u32[]{:S(2)}, u32[]{:S(2)}) %collective-permute-start.31) | collective-permute-done | bytes 32800 | tf_op jit(solution)/shard_map/ppermute | solution.py:367
  116.8 1.6 maximum_select_fusion
  118.4 1.9 collective-permute-start.3
  121.2 4.4 collective-permute-start.13
  127.8 4.0 collective-permute-start.11
  132.0 6.4 %collective-permute-done.10 = bf16[1,4,16,2560]{3,2,1,0:T(8,128)(2,1)S(1)} collective-permute-done((bf16[1,4,16,2560]{3,2,1,0:T(8,128)(2,1)S(1)}, bf16[1,4,16,2560]{3,2,1,0:T(8,128)(2,1)S(1)}, u32[]{:S(2)}, u32[]{:S(2)}) %collective-permute-start.10) | collective-permute-done | bytes 327712 | tf_op jit(solution)/shard_map/ppermute | solution.py:300
  138.4 2.5 collective-permute-start.4
  140.9 7.6 %collective-permute-start.5 = (bf16[4,1,16,2688]{3,2,1,0:T(8,128)(2,1)S(1)}, bf16[4,1,16,2688]{3,2,1,0:T(8,128)(2,1)S(1)}, u32[]{:S(2)}, u32[]{:S(2)}) collective-permute-start(bf16[4,1,16,2688]{3,2,1,0:T(8,128)(2,1)S(1)} %bitcast_dynamic-update-slice_fusion), channel_id=1, source_target_pairs={{0,2},{1,3},{2,0},{3,1},{4,6},{5,7},{6,4},{7,5},{8,10},{9,11},{10,... | collective-permute-start | bytes 1032200 | tf_op jit(solution)/shard_map/ppermute | solution.py:300
  148.5 6.6 %collective-permute-start.6 = (bf16[4,1,16,2688]{3,2,1,0:T(8,128)(2,1)S(1)}, bf16[4,1,16,2688]{3,2,1,0:T(8,128)(2,1)S(1)}, u32[]{:S(2)}, u32[]{:S(2)}) collective-permute-start(bf16[4,1,16,2688]{3,2,1,0:T(8,128)(2,1)S(1)} %bitcast_dynamic-update-slice_fusion), channel_id=1, source_target_pairs={{0,3},{1,0},{2,1},{3,2},{4,7},{5,4},{6,5},{7,6},{8,11},{9,8},{10,9... | collective-permute-start | bytes 1032200 | tf_op jit(solution)/shard_map/ppermute | solution.py:300
  156.8 4.0 collective-permute-done.5
  160.8 3.7 collective-permute-done.6
  165.6 2.0 fusion.42
  169.1 1.6 collective-permute-done.27
  173.5 2.7 collective-permute-start.21
  177.8 5.2 collective-permute-start.22
  183.5 1.6 collective-permute-start.15
  185.8 8.9 %collective-permute-start.16 = (bf16[160,256]{1,0:T(8,128)(2,1)S(1)}, bf16[160,256]{1,0:T(8,128)(2,1)S(1)}, u32[]{:S(2)}, u32[]{:S(2)}) collective-permute-start(bf16[160,256]{1,0:T(8,128)(2,1)S(1)} %get-tuple-element.6), channel_id=1, source_target_pairs={{0,8},{4,12},{8,0},{12,4},{1,9},{5,13},{9,1},{13,5},{2,10},{6,14},... | collective-permute-start | bytes 245768 | tf_op jit(solution)/shard_map/ppermute | solution.py:300
  198.0 3.3 collective-permute-start.25
  202.6 5.2 collective-permute-done.24
  207.9 2.3 collective-permute-done.25
  210.2 2.5 collective-permute-start.19
  212.8 1.8 collective-permute-done.26
  214.6 5.2 collective-permute-start.20
  220.7 4.2 collective-permute-done.19
  224.8 3.2 collective-permute-done.20
  230.0 263.4 %all-gather.2.cloned.1.call-done = bf16[64,256,128]{2,1,0:T(8,128)(2,1)} async-done(((bf16[1,256,128]{2,1,0:T(8,128)(2,1)}), bf16[64,256,128]{2,1,0:T(8,128)(2,1)}) %all-gather.2.cloned.1.call-update) | async-done | bytes 4194320 | tf_op jit(solution)/shard_map/all_gather | solution.py:371
  493.4 2.0 fusion
  497.3 18.3 %all-to-all-start.1 = ((bf16[32,16,512]{2,1,0:T(8,128)(2,1)}), bf16[32,16,512]{2,1,0:T(8,128)(2,1)S(1)}, u32[]{:S(2)}, u32[]{:S(2)}) async-start(bf16[32,16,512]{2,1,0:T(8,128)(2,1)} %bitcast.29), calls=%async_computation.1 | async-start | bytes 1048576 | tf_op jit(solution)/shard_map/all_to_all | solution.py:415
  515.6 10.9 %project.2.own_ref = bf16[256,768]{1,0:T(8,128)(2,1)} custom-call(s32[1]{0:T(128)} %bitcast.core_ref, bf16[256,8192]{1,0:T(8,128)(2,1)} %tok_ref.1, f32[1,8192]{1,0:T(1,128)} %bitcast.150, bf16[2,2048,768]{2,1,0:T(8,128)(2,1)} %bitcast.2.own_ref, bf16[2,2048,768]{2,1,0:T(8,128)(2,1)} %collective-permute-done.oth_ref), custom_call_target="tpu_custom_call" | custom-call | tf_op jit(solution)/shard_map/project/pallas_call | solution.py:136
  527.4 5.0 collective-permute-start.29
  532.4 3.2 collective-permute-done.29
  535.6 1.6 broadcast_select_fusion
  537.2 7.4 %all-to-all-start.2 = ((bf16[16,272,256]{2,1,0:T(8,128)(2,1)}), bf16[16,272,256]{2,1,0:T(8,128)(2,1)S(1)}, u32[]{:S(2)}, u32[]{:S(2)}) async-start(bf16[16,272,256]{2,1,0:T(8,128)(2,1)} %broadcast_select_fusion), calls=%async_computation.2 | async-start | bytes 4456448 | tf_op jit(solution)/shard_map/all_to_all | solution.py:342
  547.9 7.8 %project.3.img_ref = bf16[32,768]{1,0:T(8,128)(2,1)} custom-call(s32[1]{0:T(128)} %bitcast.core_ref, bf16[32,8192]{1,0:T(8,128)(2,1)} %reshape.346.x_ref.img_ref, f32[1,8192]{1,0:T(1,128)} %bitcast.151, bf16[2,2048,768]{2,1,0:T(8,128)(2,1)} %bitcast.2.own_ref, bf16[2,2048,768]{2,1,0:T(8,128)(2,1)} %collective-permute-done.oth_ref), custom_call_target="tpu_custom_call" | custom-call | tf_op jit(solution)/shard_map/project/pallas_call | solution.py:136
  556.5 5.9 collective-permute-start.30
  565.0 10.0 %all-to-all-done.2.kv_ref = bf16[16,272,256]{2,1,0:T(8,128)(2,1)S(1)} async-done(((bf16[16,272,256]{2,1,0:T(8,128)(2,1)}), bf16[16,272,256]{2,1,0:T(8,128)(2,1)S(1)}, u32[]{:S(2)}, u32[]{:S(2)}) %all-to-all-start.2) | async-done | bytes 2228256 | tf_op jit(solution)/shard_map/all_to_all | solution.py:342
  575.0 5.3 all-to-all-start.3
  582.1 5.2 all-to-all-done.3
  588.0 22.8 %attention.1.att_ref = bf16[256,512]{1,0:T(8,128)(2,1)} custom-call(bf16[256,768]{1,0:T(8,128)(2,1)} %project.2.own_ref, bf16[32,768]{1,0:T(8,128)(2,1)} %project.3.img_ref, bf16[16,272,256]{2,1,0:T(8,128)(2,1)} %copy-done, bf16[512,256]{1,0:T(8,128)(2,1)} %bitcast.147, s32[256,1]{1,0:T(8,128)} %copy.45.index_ref, s32[256,1]{1,0:T(8,128)} %iota_add_fusion.qpos_ref, ...), custom_call_target="tpu_custom_call" | custom-call | tf_op jit(solution)/shard_map/attention/pallas_call | solution.py:213
  610.7 11.2 %output_layer.1 = bf16[256,8192]{1,0:T(8,128)(2,1)} custom-call(s32[1]{0:T(128)} %bitcast.core_ref, bf16[256,512]{1,0:T(8,128)(2,1)} %attention.1.att_ref, bf16[256,8192]{1,0:T(8,128)(2,1)} %tok_ref.1, bf16[32,8192]{1,0:T(8,128)(2,1)} %reshape.346.x_ref.img_ref, s32[256,1]{1,0:T(8,128)} %copy.45.index_ref, bf16[2,16,512,128]{3,2,1,0:T(8,128)(2,1)} %bitcast.136, ...), custom_call_target="tpu_custom_call" | custom-call | tf_op jit(solution)/shard_map/output_layer/pallas_call | solution.py:264
  (169 shorter events, 41.5 us)
Async XLA Ops:
  10.5 16.5 %copy-start.12 = (s32[16]{0:T(128)S(1)}, s32[16]{0:T(128)}, u32[]{:S(2)}) copy-start(s32[16]{0:T(128)} %param.23) | copy-start | bytes 196
  10.5 18.6 %copy-start.9 = (bf16[64,768]{1,0:T(8,128)(2,1)S(1)}, bf16[64,768]{1,0:T(8,128)(2,1)}, u32[]{:S(2)}) copy-start(bf16[64,768]{1,0:T(8,128)(2,1)} %param.28) | copy-start | bytes 294916
  21.1 97.3 %collective-permute-start.7 = (bf16[16,2560]{1,0:T(8,128)(2,1)S(1)}, bf16[16,2560]{1,0:T(8,128)(2,1)}, u32[]{:S(2)}, u32[]{:S(2)}) collective-permute-start(bf16[16,2560]{1,0:T(8,128)(2,1)S(1)} %get-tuple-element.13), channel_id=1, source_target_pairs={{0,1},{1,2},{2,3},{3,0},{4,5},{5,6},{6,7},{7,4},{8,9},{9,10},{10,1... | collective-permute-start | bytes 245768 | tf_op jit(solution)/shard_map/ppermute | solution.py:300
  22.7 98.5 %collective-permute-start.8 = (bf16[16,2560]{1,0:T(8,128)(2,1)S(1)}, bf16[16,2560]{1,0:T(8,128)(2,1)}, u32[]{:S(2)}, u32[]{:S(2)}) collective-permute-start(bf16[16,2560]{1,0:T(8,128)(2,1)S(1)} %get-tuple-element.13), channel_id=1, source_target_pairs={{0,2},{1,3},{2,0},{3,1},{4,6},{5,7},{6,4},{7,5},{8,10},{9,11},{10,... | collective-permute-start | bytes 245768 | tf_op jit(solution)/shard_map/ppermute | solution.py:300
  25.6 100.9 %collective-permute-start.9 = (bf16[16,2560]{1,0:T(8,128)(2,1)S(1)}, bf16[16,2560]{1,0:T(8,128)(2,1)}, u32[]{:S(2)}, u32[]{:S(2)}) collective-permute-start(bf16[16,2560]{1,0:T(8,128)(2,1)S(1)} %get-tuple-element.13), channel_id=1, source_target_pairs={{0,3},{1,0},{2,1},{3,2},{4,7},{5,4},{6,5},{7,6},{8,11},{9,8},{10,9... | collective-permute-start | bytes 245768 | tf_op jit(solution)/shard_map/ppermute | solution.py:300
  27.1 100.6 %collective-permute-start.1 = (bf16[16,2688]{1,0:T(8,128)(2,1)S(1)}, bf16[16,2688]{1,0:T(8,128)(2,1)S(1)}, u32[]{:S(2)}, u32[]{:S(2)}) collective-permute-start(bf16[16,2688]{1,0:T(8,128)(2,1)S(1)} %pad_maximum_fusion.1), channel_id=1, source_target_pairs={{0,4},{4,8},{8,12},{12,0},{1,5},{5,9},{9,13},{13,1},{2,6},{6,10},{... | collective-permute-start | bytes 258056 | tf_op jit(solution)/shard_map/ppermute | solution.py:300
  32.5 8.6 %copy-start.10 = (bf16[512,64]{0,1:T(8,128)(2,1)S(1)}, bf16[512,64]{0,1:T(8,128)(2,1)}, u32[]{:S(2)}) copy-start(bf16[512,64]{0,1:T(8,128)(2,1)} %param.29) | copy-start | bytes 196612
  32.5 13.1 %copy-start.6 = (bf16[5120,256]{1,0:T(8,128)(2,1)S(1)}, bf16[5120,256]{1,0:T(8,128)(2,1)}, u32[]{:S(2)}) copy-start(bf16[5120,256]{1,0:T(8,128)(2,1)} %param.22) | copy-start | bytes 7864324
  32.5 132.6 %all-to-all-start = ((bf16[64,64,768]{2,1,0:T(8,128)(2,1)}), bf16[64,64,768]{2,1,0:T(8,128)(2,1)}, u32[]{:S(2)}, u32[]{:S(2)}) async-start(bf16[64,64,768]{2,1,0:T(8,128)(2,1)} %broadcast_in_dim.219), calls=%async_computation | async-start | bytes 12582912 | tf_op jit(solution)/shard_map/all_to_all | solution.py:324
  41.0 452.3 %all-gather.2.cloned.1.call-start = ((), (), s32[]{:S(2)}) async-start(), calls=%async_computation.4 | async-start | bytes 4259840 | tf_op jit(solution)/shard_map/all_gather | solution.py:371
  42.0 74.5 %collective-permute-start.31 = (bf16[256,64]{1,0:T(8,128)(2,1)}, bf16[256,64]{1,0:T(8,128)(2,1)}, u32[]{:S(2)}, u32[]{:S(2)}) collective-permute-start(bf16[256,64]{1,0:T(8,128)(2,1)} %get-tuple-element.15), channel_id=1, source_target_pairs={{0,1},{1,0},{2,3},{3,2},{4,5},{5,4},{6,7},{7,6},{8,9},{9,8},{10,11... | collective-permute-start | bytes 98312 | tf_op jit(solution)/shard_map/ppermute | solution.py:367
  116.5 11.3 %collective-permute-start.2 = (bf16[16,2688]{1,0:T(8,128)(2,1)S(1)}, bf16[16,2688]{1,0:T(8,128)(2,1)S(1)}, u32[]{:S(2)}, u32[]{:S(2)}) collective-permute-start(bf16[16,2688]{1,0:T(8,128)(2,1)S(1)} %pad_maximum_fusion.1), channel_id=1, source_target_pairs={{0,8},{4,12},{8,0},{12,4},{1,9},{5,13},{9,1},{13,5},{2,10},{6,14},... | collective-permute-start | bytes 258056 | tf_op jit(solution)/shard_map/ppermute | solution.py:300
  118.4 13.3 %collective-permute-start.3 = (bf16[16,2688]{1,0:T(8,128)(2,1)S(1)}, bf16[16,2688]{1,0:T(8,128)(2,1)S(1)}, u32[]{:S(2)}, u32[]{:S(2)}) collective-permute-start(bf16[16,2688]{1,0:T(8,128)(2,1)S(1)} %pad_maximum_fusion.1), channel_id=1, source_target_pairs={{0,12},{4,0},{8,4},{12,8},{1,13},{5,1},{9,5},{13,9},{2,14},{6,2},{... | collective-permute-start | bytes 258056 | tf_op jit(solution)/shard_map/ppermute | solution.py:300
  121.2 43.5 %collective-permute-start.13 = (bf16[160,2560]{1,0:T(8,128)(2,1)}, bf16[160,2560]{1,0:T(8,128)(2,1)}, u32[]{:S(2)}, u32[]{:S(2)}) collective-permute-start(bf16[160,2560]{1,0:T(8,128)(2,1)} %dynamic-slice_bitcast_fusion), channel_id=1, source_target_pairs={{0,16},{16,0},{1,17},{17,1},{2,18},{18,2},{3,19},{19,3},{4,20},{20... | collective-permute-start | bytes 2457608 | tf_op jit(solution)/shard_map/ppermute | solution.py:292
  126.5 44.1 %collective-permute-start.27 = (bf16[2560,256]{1,0:T(8,128)(2,1)}, bf16[2560,256]{1,0:T(8,128)(2,1)}, u32[]{:S(2)}, u32[]{:S(2)}) collective-permute-start(bf16[2560,256]{1,0:T(8,128)(2,1)} %constant_dynamic-slice_fusion), channel_id=1, source_target_pairs={{0,16},{16,0},{1,17},{17,1},{2,18},{18,2},{3,19},{19,3},{4,20},{20... | collective-permute-start | bytes 3932168 | tf_op jit(solution)/shard_map/ppermute | solution.py:292
  127.7 10.7 %collective-permute-start.10 = (bf16[1,4,16,2560]{3,2,1,0:T(8,128)(2,1)S(1)}, bf16[1,4,16,2560]{3,2,1,0:T(8,128)(2,1)S(1)}, u32[]{:S(2)}, u32[]{:S(2)}) collective-permute-start(bf16[1,4,16,2560]{3,2,1,0:T(8,128)(2,1)S(1)} %bitcast_dynamic-update-slice_fusion.12), channel_id=1, source_target_pairs={{0,4},{4,8},{8,12},{12,0},{1,5},{5,9},{9,13},{13,1},{2,6},{6,10},{... | collective-permute-start | bytes 983048 | tf_op jit(solution)/shard_map/ppermute | solution.py:300
  127.8 13.1 %collective-permute-start.11 = (bf16[1,4,16,2560]{3,2,1,0:T(8,128)(2,1)S(1)}, bf16[1,4,16,2560]{3,2,1,0:T(8,128)(2,1)S(1)}, u32[]{:S(2)}, u32[]{:S(2)}) collective-permute-start(bf16[1,4,16,2560]{3,2,1,0:T(8,128)(2,1)S(1)} %bitcast_dynamic-update-slice_fusion.12), channel_id=1, source_target_pairs={{0,8},{4,12},{8,0},{12,4},{1,9},{5,13},{9,1},{13,5},{2,10},{6,14},... | collective-permute-start | bytes 983048 | tf_op jit(solution)/shard_map/ppermute | solution.py:300
  131.8 16.8 %collective-permute-start.12 = (bf16[1,4,16,2560]{3,2,1,0:T(8,128)(2,1)S(1)}, bf16[1,4,16,2560]{3,2,1,0:T(8,128)(2,1)S(1)}, u32[]{:S(2)}, u32[]{:S(2)}) collective-permute-start(bf16[1,4,16,2560]{3,2,1,0:T(8,128)(2,1)S(1)} %bitcast_dynamic-update-slice_fusion.12), channel_id=1, source_target_pairs={{0,12},{4,0},{8,4},{12,8},{1,13},{5,1},{9,5},{13,9},{2,14},{6,2},{... | collective-permute-start | bytes 983048 | tf_op jit(solution)/shard_map/ppermute | solution.py:300
  132.0 23.2 %copy-start.8 = (bf16[5120,160]{0,1:T(8,128)(2,1)S(1)}, bf16[5120,160]{0,1:T(8,128)(2,1)}, u32[]{:S(2)}) copy-start(bf16[5120,160]{0,1:T(8,128)(2,1)} %param.21) | copy-start | bytes 4915204
  138.4 18.4 %collective-permute-start.4 = (bf16[4,1,16,2688]{3,2,1,0:T(8,128)(2,1)S(1)}, bf16[4,1,16,2688]{3,2,1,0:T(8,128)(2,1)S(1)}, u32[]{:S(2)}, u32[]{:S(2)}) collective-permute-start(bf16[4,1,16,2688]{3,2,1,0:T(8,128)(2,1)S(1)} %bitcast_dynamic-update-slice_fusion), channel_id=1, source_target_pairs={{0,1},{1,2},{2,3},{3,0},{4,5},{5,6},{6,7},{7,4},{8,9},{9,10},{10,1... | collective-permute-start | bytes 1032200 | tf_op jit(solution)/shard_map/ppermute | solution.py:300
  140.9 19.9 %collective-permute-start.5 = (bf16[4,1,16,2688]{3,2,1,0:T(8,128)(2,1)S(1)}, bf16[4,1,16,2688]{3,2,1,0:T(8,128)(2,1)S(1)}, u32[]{:S(2)}, u32[]{:S(2)}) collective-permute-start(bf16[4,1,16,2688]{3,2,1,0:T(8,128)(2,1)S(1)} %bitcast_dynamic-update-slice_fusion), channel_id=1, source_target_pairs={{0,2},{1,3},{2,0},{3,1},{4,6},{5,7},{6,4},{7,5},{8,10},{9,11},{10,... | collective-permute-start | bytes 1032200 | tf_op jit(solution)/shard_map/ppermute | solution.py:300
  148.5 16.0 %collective-permute-start.6 = (bf16[4,1,16,2688]{3,2,1,0:T(8,128)(2,1)S(1)}, bf16[4,1,16,2688]{3,2,1,0:T(8,128)(2,1)S(1)}, u32[]{:S(2)}, u32[]{:S(2)}) collective-permute-start(bf16[4,1,16,2688]{3,2,1,0:T(8,128)(2,1)S(1)} %bitcast_dynamic-update-slice_fusion), channel_id=1, source_target_pairs={{0,3},{1,0},{2,1},{3,2},{4,7},{5,4},{6,5},{7,6},{8,11},{9,8},{10,9... | collective-permute-start | bytes 1032200 | tf_op jit(solution)/shard_map/ppermute | solution.py:300
  164.7 6.0 collective-permute-start.14
  165.1 350.5 %collective-permute-start = (bf16[2,2048,768]{2,1,0:T(8,128)(2,1)}, bf16[2,2048,768]{2,1,0:T(8,128)(2,1)}, u32[]{:S(2)}, u32[]{:S(2)}) collective-permute-start(bf16[2,2048,768]{2,1,0:T(8,128)(2,1)} %bitcast.2.own_ref), channel_id=1, source_target_pairs={{0,32},{32,0},{1,33},{33,1},{2,34},{34,2},{3,35},{35,3},{4,36},{36... | collective-permute-start | bytes 18874376 | tf_op jit(solution)/shard_map/ppermute | solution.py:292
  170.7 59.2 %collective-permute-start.28 = (bf16[2560,256]{1,0:T(8,128)(2,1)}, bf16[2560,256]{1,0:T(8,128)(2,1)S(1)}, u32[]{:S(2)}, u32[]{:S(2)}) collective-permute-start(bf16[2560,256]{1,0:T(8,128)(2,1)} %collective-permute-done.27), channel_id=1, source_target_pairs={{0,32},{32,0},{1,33},{33,1},{2,34},{34,2},{3,35},{35,3},{4,36},{36... | collective-permute-start | bytes 3932168 | tf_op jit(solution)/shard_map/ppermute | solution.py:292
  173.5 10.1 %collective-permute-start.21 = (bf16[160,256]{1,0:T(8,128)(2,1)S(1)}, bf16[160,256]{1,0:T(8,128)(2,1)S(1)}, u32[]{:S(2)}, u32[]{:S(2)}) collective-permute-start(bf16[160,256]{1,0:T(8,128)(2,1)S(1)} %get-tuple-element.12), channel_id=1, source_target_pairs={{0,1},{1,2},{2,3},{3,0},{4,5},{5,6},{6,7},{7,4},{8,9},{9,10},{10,1... | collective-permute-start | bytes 245768 | tf_op jit(solution)/shard_map/ppermute | solution.py:300
  177.8 8.1 %collective-permute-start.22 = (bf16[160,256]{1,0:T(8,128)(2,1)S(1)}, bf16[160,256]{1,0:T(8,128)(2,1)S(1)}, u32[]{:S(2)}, u32[]{:S(2)}) collective-permute-start(bf16[160,256]{1,0:T(8,128)(2,1)S(1)} %get-tuple-element.12), channel_id=1, source_target_pairs={{0,2},{1,3},{2,0},{3,1},{4,6},{5,7},{6,4},{7,5},{8,10},{9,11},{10,... | collective-permute-start | bytes 245768 | tf_op jit(solution)/shard_map/ppermute | solution.py:300
  183.0 11.8 %collective-permute-start.23 = (bf16[160,256]{1,0:T(8,128)(2,1)S(1)}, bf16[160,256]{1,0:T(8,128)(2,1)S(1)}, u32[]{:S(2)}, u32[]{:S(2)}) collective-permute-start(bf16[160,256]{1,0:T(8,128)(2,1)S(1)} %get-tuple-element.12), channel_id=1, source_target_pairs={{0,3},{1,0},{2,1},{3,2},{4,7},{5,4},{6,5},{7,6},{8,11},{9,8},{10,9... | collective-permute-start | bytes 245768 | tf_op jit(solution)/shard_map/ppermute | solution.py:300
  183.5 12.2 %collective-permute-start.15 = (bf16[160,256]{1,0:T(8,128)(2,1)S(1)}, bf16[160,256]{1,0:T(8,128)(2,1)S(1)}, u32[]{:S(2)}, u32[]{:S(2)}) collective-permute-start(bf16[160,256]{1,0:T(8,128)(2,1)S(1)} %get-tuple-element.6), channel_id=1, source_target_pairs={{0,4},{4,8},{8,12},{12,0},{1,5},{5,9},{9,13},{13,1},{2,6},{6,10},{... | collective-permute-start | bytes 245768 | tf_op jit(solution)/shard_map/ppermute | solution.py:300
  185.8 12.2 %collective-permute-start.16 = (bf16[160,256]{1,0:T(8,128)(2,1)S(1)}, bf16[160,256]{1,0:T(8,128)(2,1)S(1)}, u32[]{:S(2)}, u32[]{:S(2)}) collective-permute-start(bf16[160,256]{1,0:T(8,128)(2,1)S(1)} %get-tuple-element.6), channel_id=1, source_target_pairs={{0,8},{4,12},{8,0},{12,4},{1,9},{5,13},{9,1},{13,5},{2,10},{6,14},... | collective-permute-start | bytes 245768 | tf_op jit(solution)/shard_map/ppermute | solution.py:300
  194.8 6.6 %collective-permute-start.17 = (bf16[160,256]{1,0:T(8,128)(2,1)S(1)}, bf16[160,256]{1,0:T(8,128)(2,1)S(1)}, u32[]{:S(2)}, u32[]{:S(2)}) collective-permute-start(bf16[160,256]{1,0:T(8,128)(2,1)S(1)} %get-tuple-element.6), channel_id=1, source_target_pairs={{0,12},{4,0},{8,4},{12,8},{1,13},{5,1},{9,5},{13,9},{2,14},{6,2},{... | collective-permute-start | bytes 245768 | tf_op jit(solution)/shard_map/ppermute | solution.py:300
  195.7 12.1 %collective-permute-start.24 = (bf16[1,4,160,256]{3,2,1,0:T(8,128)(2,1)S(1)}, bf16[1,4,160,256]{3,2,1,0:T(8,128)(2,1)S(1)}, u32[]{:S(2)}, u32[]{:S(2)}) collective-permute-start(bf16[1,4,160,256]{3,2,1,0:T(8,128)(2,1)S(1)} %bitcast_dynamic-update-slice_fusion.4), channel_id=1, source_target_pairs={{0,4},{4,8},{8,12},{12,0},{1,5},{5,9},{9,13},{13,1},{2,6},{6,10},{... | collective-permute-start | bytes 983048 | tf_op jit(solution)/shard_map/ppermute | solution.py:300
  198.0 12.2 %collective-permute-start.25 = (bf16[1,4,160,256]{3,2,1,0:T(8,128)(2,1)S(1)}, bf16[1,4,160,256]{3,2,1,0:T(8,128)(2,1)S(1)}, u32[]{:S(2)}, u32[]{:S(2)}) collective-permute-start(bf16[1,4,160,256]{3,2,1,0:T(8,128)(2,1)S(1)} %bitcast_dynamic-update-slice_fusion.4), channel_id=1, source_target_pairs={{0,8},{4,12},{8,0},{12,4},{1,9},{5,13},{9,1},{13,5},{2,10},{6,14},... | collective-permute-start | bytes 983048 | tf_op jit(solution)/shard_map/ppermute | solution.py:300
  201.4 13.2 %collective-permute-start.26 = (bf16[1,4,160,256]{3,2,1,0:T(8,128)(2,1)S(1)}, bf16[1,4,160,256]{3,2,1,0:T(8,128)(2,1)S(1)}, u32[]{:S(2)}, u32[]{:S(2)}) collective-permute-start(bf16[1,4,160,256]{3,2,1,0:T(8,128)(2,1)S(1)} %bitcast_dynamic-update-slice_fusion.4), channel_id=1, source_target_pairs={{0,12},{4,0},{8,4},{12,8},{1,13},{5,1},{9,5},{13,9},{2,14},{6,2},{... | collective-permute-start | bytes 983048 | tf_op jit(solution)/shard_map/ppermute | solution.py:300
  207.9 12.8 %collective-permute-start.18 = (bf16[4,1,160,256]{3,2,1,0:T(8,128)(2,1)S(1)}, bf16[4,1,160,256]{3,2,1,0:T(8,128)(2,1)S(1)}, u32[]{:S(2)}, u32[]{:S(2)}) collective-permute-start(bf16[4,1,160,256]{3,2,1,0:T(8,128)(2,1)S(1)} %bitcast_dynamic-update-slice_fusion.8), channel_id=1, source_target_pairs={{0,1},{1,2},{2,3},{3,0},{4,5},{5,6},{6,7},{7,4},{8,9},{9,10},{10,1... | collective-permute-start | bytes 983048 | tf_op jit(solution)/shard_map/ppermute | solution.py:300
  210.2 14.6 %collective-permute-start.19 = (bf16[4,1,160,256]{3,2,1,0:T(8,128)(2,1)S(1)}, bf16[4,1,160,256]{3,2,1,0:T(8,128)(2,1)S(1)}, u32[]{:S(2)}, u32[]{:S(2)}) collective-permute-start(bf16[4,1,160,256]{3,2,1,0:T(8,128)(2,1)S(1)} %bitcast_dynamic-update-slice_fusion.8), channel_id=1, source_target_pairs={{0,2},{1,3},{2,0},{3,1},{4,6},{5,7},{6,4},{7,5},{8,10},{9,11},{10,... | collective-permute-start | bytes 983048 | tf_op jit(solution)/shard_map/ppermute | solution.py:300
  212.8 15.4 %copy-start.7 = (bf16[5120,256]{1,0:T(8,128)(2,1)S(1)}, bf16[5120,256]{1,0:T(8,128)(2,1)}, u32[]{:S(2)}) copy-start(bf16[5120,256]{1,0:T(8,128)(2,1)} %param.22) | copy-start | bytes 7864324
  214.6 13.5 %collective-permute-start.20 = (bf16[4,1,160,256]{3,2,1,0:T(8,128)(2,1)S(1)}, bf16[4,1,160,256]{3,2,1,0:T(8,128)(2,1)S(1)}, u32[]{:S(2)}, u32[]{:S(2)}) collective-permute-start(bf16[4,1,160,256]{3,2,1,0:T(8,128)(2,1)S(1)} %bitcast_dynamic-update-slice_fusion.8), channel_id=1, source_target_pairs={{0,3},{1,0},{2,1},{3,2},{4,7},{5,4},{6,5},{7,6},{8,11},{9,8},{10,9... | collective-permute-start | bytes 983048 | tf_op jit(solution)/shard_map/ppermute | solution.py:300
  219.9 8.9 %copy-start.3 = (bf16[4,4,160,256]{3,2,1,0:T(8,128)(2,1)}, bf16[4,4,160,256]{3,2,1,0:T(8,128)(2,1)S(1)}, u32[]{:S(2)}) copy-start(bf16[4,4,160,256]{3,2,1,0:T(8,128)(2,1)S(1)} %constant_dynamic-update-slice_fusion.2) | copy-start | bytes 3932164
  493.4 2.1 copy-start.2
  493.4 117.4 %collective-permute-start.32 = (bf16[2,16,512,128]{3,2,1,0:T(8,128)(2,1)}, bf16[2,16,512,128]{3,2,1,0:T(8,128)(2,1)}, u32[]{:S(2)}, u32[]{:S(2)}) collective-permute-start(bf16[2,16,512,128]{3,2,1,0:T(8,128)(2,1)} %bitcast.135), channel_id=1, source_target_pairs={{0,32},{32,0},{1,33},{33,1},{2,34},{34,2},{3,35},{35,3},{4,36},{36... | collective-permute-start | bytes 12582920 | tf_op jit(solution)/shard_map/ppermute | solution.py:292
  497.3 40.0 %all-to-all-start.1 = ((bf16[32,16,512]{2,1,0:T(8,128)(2,1)}), bf16[32,16,512]{2,1,0:T(8,128)(2,1)S(1)}, u32[]{:S(2)}, u32[]{:S(2)}) async-start(bf16[32,16,512]{2,1,0:T(8,128)(2,1)} %bitcast.29), calls=%async_computation.1 | async-start | bytes 1048576 | tf_op jit(solution)/shard_map/all_to_all | solution.py:415
  527.4 8.2 %collective-permute-start.29 = (bf16[272,256]{1,0:T(8,128)(2,1)S(1)}, bf16[272,256]{1,0:T(8,128)(2,1)S(1)}, u32[]{:S(2)}, u32[]{:S(2)}) collective-permute-start(bf16[272,256]{1,0:T(8,128)(2,1)S(1)} %pad_maximum_fusion), channel_id=1, source_target_pairs={{0,16},{1,17},{2,18},{3,19},{4,20},{5,21},{6,22},{7,23},{8,24},{9,... | collective-permute-start | bytes 417800 | tf_op jit(solution)/shard_map/ppermute | solution.py:337
  537.2 7.5 %copy-start.13 = (s32[1,4]{1,0:T(1,128)S(1)}, s32[1,4]{1,0:T(1,128)}, u32[]{:S(2)}) copy-start(s32[1,4]{1,0:T(1,128)} %param.26) | copy-start | bytes 52
  537.2 37.8 %all-to-all-start.2 = ((bf16[16,272,256]{2,1,0:T(8,128)(2,1)}), bf16[16,272,256]{2,1,0:T(8,128)(2,1)S(1)}, u32[]{:S(2)}, u32[]{:S(2)}) async-start(bf16[16,272,256]{2,1,0:T(8,128)(2,1)} %broadcast_select_fusion), calls=%async_computation.2 | async-start | bytes 4456448 | tf_op jit(solution)/shard_map/all_to_all | solution.py:342
  556.5 7.7 %collective-permute-start.30 = (bf16[32,256]{1,0:T(8,128)(2,1)S(1)}, bf16[32,256]{1,0:T(8,128)(2,1)S(1)}, u32[]{:S(2)}, u32[]{:S(2)}) collective-permute-start(bf16[32,256]{1,0:T(8,128)(2,1)S(1)} %slice.80), channel_id=1, source_target_pairs={{0,16},{1,17},{2,18},{3,19},{4,20},{5,21},{6,22},{7,23},{8,24},{9,... | collective-permute-start | bytes 49160 | tf_op jit(solution)/shard_map/ppermute | solution.py:337
  575.0 12.2 %copy-start = (bf16[16,272,256]{2,1,0:T(8,128)(2,1)}, bf16[16,272,256]{2,1,0:T(8,128)(2,1)S(1)}, u32[]{:S(2)}) copy-start(bf16[16,272,256]{2,1,0:T(8,128)(2,1)S(1)} %all-to-all-done.2.kv_ref) | copy-start | bytes 6684676
  575.0 12.2 %all-to-all-start.3 = ((bf16[16,32,256]{2,1,0:T(8,128)(2,1)}), bf16[16,32,256]{2,1,0:T(8,128)(2,1)S(1)}, u32[]{:S(2)}, u32[]{:S(2)}) async-start(bf16[16,32,256]{2,1,0:T(8,128)(2,1)} %broadcast_select_fusion.1), calls=%async_computation.3 | async-start | bytes 524288 | tf_op jit(solution)/shard_map/all_to_all | solution.py:342
  (4 other events, 4.3 us)
Sparse Core Ops, SparseCore 0:
  118.5 374.7 all-gather.1
